TPU v7x, 32 devices: a whole 2x2x4 slice. The times are simulated.
32 devices in a mesh: dp: 8 (over y, x, core), mp: 4 (over z).
Axes of the slice: x: 2, y: 2, z: 4, core: 2. Of those that a mesh axis runs over, the one named last changes fastest.
Arguments:
- tokens: bfloat16 [2048, 4096], P('dp'), may hold values from -6 to 6
- pack_source: int32 [2048], P('dp'), may hold values from 0 to 2047, as said below
- segment_ids: int32 [2048], P('dp'), may hold values from 0 to 3, never falling along the last dimension, each value on 1 to 1536 neighbouring positions
- w_in: bfloat16 [4096, 20480], P('dp', 'mp'), may hold values from -0.09375 to 0.09375
- w_dt: bfloat16 [4096, 128], P('dp', 'mp'), may hold values from -0.09375 to 0.09375
- w_out: bfloat16 [4096, 8192], P(None, 'mp'), may hold values from -0.0625 to 0.0625
- conv_x: float32 [4, 8192], P(None, 'mp'), may hold values from -3 to 3
- conv_bc: float32 [4, 2, 2048], P(None, None, 'mp'), may hold values from -3 to 3
- dt_bias: float32 [128], P('mp'), may hold values from -5 to -3
- decay_rate: float32 [128], P('mp'), may hold values from 0.0625 to 0.5
- skip_gain: float32 [128], P('mp'), may hold values from 0.1 to 0.5
- norm_gain: float32 [8192], P('mp'), may hold values from 0.1 to 1.9
Outputs:
- mixed: bfloat16 [2048, 4096], P(('dp', 'mp'))
Inputs may be any that keep to these rules, and one draw needn't show every extreme that they name: pack_source is a permutation of the generation-order rows. Taking aligned blocks of 256 rows on both sides, a block of packed positions holds at most 64 rows of any one block of generation-order rows; each packed block holds exactly 64 rows of exactly one generation block, and each generation block gives exactly 64 rows to exactly one packed block. `segment_ids`: non-decreasing; each response has 1 to 1536 positions and one has exactly 1536.
All inputs are finite; a program needn't handle non-finite values.
Results may differ from a plain program's by a relative error of at most 0.012.
Values may be sent and summed in bfloat16 or wider, within the bound.
A program may use at most 192 MiB of HBM per device.

v0:
```python
import jax
import jax.numpy as jnp
from jax import lax
from jax.sharding import PartitionSpec as P

HEAD_DIM = 64
STATE = 256
CONV = 4
BLOCK = 256


highest = lax.Precision.HIGHEST


def passed_along(x, axis, by):
    size = lax.axis_size(axis)
    pairs = [(i, i + by) for i in range(size) if 0 <= i + by < size]
    return lax.ppermute(x, axis, pairs)


def carried_in(x, axis, join, neutral):
    place = lax.axis_index(axis)
    gathered = jax.tree.map(
        lambda a, kind: lax.all_gather(a.astype(kind), axis), x, (jnp.bfloat16, jnp.bfloat16)
    )
    state = jax.tree.map(lambda a, e: jnp.zeros_like(a) + jnp.asarray(e, a.dtype), x, neutral)

    def one(hop, state):
        return join(
            state,
            jax.tree.map(
                lambda a, own: lax.dynamic_index_in_dim(a, hop, 0, False).astype(own.dtype),
                gathered,
                x,
            ),
        )

    return lax.fori_loop(0, place, one, state)


def chain_combine(earlier, later_part):
    return (earlier[0] * later_part[0], later_part[0][:, None, None] * earlier[1] + later_part[1])


def block_step(carry, pieces):
    state_now, prev_seg = carry
    x_block, b_block, c_block, step_dt, step_rate, seg_block = pieces
    per_group = x_block.shape[1] // b_block.shape[1]
    cum_rate = jnp.cumsum(step_rate, axis=0)
    places = jnp.arange(seg_block.shape[0])
    linked = (seg_block[:, None] == seg_block[None, :]) & (places[:, None] >= places[None, :])
    log_spans = cum_rate.T[:, :, None] - cum_rate.T[:, None, :]
    decay_mat = jnp.where(linked[None], jnp.exp(jnp.where(linked[None], log_spans, 0.0)), 0.0)
    scores = jnp.einsum("tgn,sgn->gts", c_block, b_block, preferred_element_type=jnp.float32)
    scores = jnp.repeat(scores, per_group, axis=0)
    mixing = (scores * decay_mat * step_dt.T[:, None, :]).astype(jnp.bfloat16)
    in_block = jnp.einsum("hts,shp->thp", mixing, x_block, preferred_element_type=jnp.float32)
    c_heads = jnp.repeat(c_block.astype(jnp.float32), per_group, axis=1)
    b_heads = jnp.repeat(b_block.astype(jnp.float32), per_group, axis=1)
    entry_mask = jnp.where((seg_block == prev_seg)[:, None], jnp.exp(cum_rate), 0.0)
    from_before = entry_mask[:, :, None] * jnp.einsum(
        "thn,hpn->thp", c_heads, state_now, precision=highest
    )
    last_seg = seg_block[-1]
    weight = (
        jnp.where((seg_block == last_seg)[:, None], jnp.exp(cum_rate[-1][None, :] - cum_rate), 0.0)
        * step_dt
    )
    carried = jnp.where(last_seg == prev_seg, jnp.exp(cum_rate[-1]), 0.0)
    added_in = jnp.einsum(
        "shp,shn->hpn", weight[:, :, None] * x_block.astype(jnp.float32), b_heads, precision=highest
    )
    return ((carried[:, None, None] * state_now + added_in, last_seg), in_block + from_before)


def on_device(
    tokens,
    pack_source,
    segment_ids,
    w_in,
    w_dt,
    w_out,
    conv_x,
    conv_bc,
    dt_bias,
    decay_rate,
    skip_gain,
    norm_gain,
):
    row_count = tokens.shape[0]
    data_devs = lax.axis_size("dp")
    capacity = 2 * row_count // data_devs
    source_dev = pack_source // row_count
    source_row = pack_source % row_count
    same_source = source_dev[:, None] == source_dev[None, :]
    earlier_rows = pack_source[None, :] < pack_source[:, None]
    rank_in = jnp.sum((same_source & earlier_rows).astype(jnp.int32), axis=1)
    slot_index = source_dev * capacity + rank_in
    requests = (
        jnp.full((data_devs * capacity,), -1, jnp.int32)
        .at[slot_index]
        .set(source_row)
        .reshape(data_devs, capacity)
    )
    wanted = lax.all_to_all(requests, "dp", split_axis=0, concat_axis=0, tiled=True)
    fetched = jnp.where(
        (wanted >= 0)[:, :, None], tokens[jnp.maximum(wanted, 0)], jnp.zeros((), jnp.bfloat16)
    )
    replies = lax.all_to_all(fetched, "dp", split_axis=0, concat_axis=0, tiled=True)
    gathered = replies.reshape(data_devs * capacity, tokens.shape[1])[slot_index]
    panel_cols = w_in.shape[1]
    head_count = w_dt.shape[1]
    chan_width = w_out.shape[1]
    proj_sum = jnp.dot(
        gathered, lax.all_gather(w_in, "dp", axis=0, tiled=True), preferred_element_type=jnp.float32
    )
    step_sum = jnp.dot(
        gathered, lax.all_gather(w_dt, "dp", axis=0, tiled=True), preferred_element_type=jnp.float32
    )
    proj_sum, dt_raw = (proj_sum, step_sum)
    projected = proj_sum.astype(jnp.bfloat16)
    group_width = (panel_cols - 2 * chan_width) // 2
    gate_in = projected[:, chan_width : 2 * chan_width]
    stacked = jnp.concatenate([projected[:, :chan_width], projected[:, 2 * chan_width :]], axis=1)
    tail_len = CONV - 1
    tail_vals = stacked[row_count - tail_len :].astype(jnp.float32)
    tail_seg = (segment_ids[row_count - tail_len :] + 1).astype(jnp.float32)
    prev_vals, prev_seg = passed_along((tail_vals, tail_seg), "dp", 1)
    extended = jnp.concatenate([prev_vals.astype(jnp.bfloat16), stacked], axis=0)
    seg_ext = jnp.concatenate([prev_seg.astype(jnp.int32) - 1, segment_ids], axis=0)
    kernel = jnp.concatenate([conv_x, conv_bc.reshape(CONV, 2 * group_width)], axis=1)
    conv_sum = jnp.zeros((row_count, stacked.shape[1]), jnp.float32)
    for lag_index in range(CONV):
        same_seg = (seg_ext[lag_index : lag_index + row_count] == segment_ids)[:, None]
        conv_sum = conv_sum + jnp.where(
            same_seg,
            kernel[lag_index][None, :]
            * extended[lag_index : lag_index + row_count].astype(jnp.float32),
            0.0,
        )
    convolved = jax.nn.silu(conv_sum).astype(jnp.bfloat16)
    local_groups = group_width // STATE
    x_all = convolved[:, :chan_width].reshape(row_count, head_count, HEAD_DIM)
    b_all = convolved[:, chan_width : chan_width + group_width].reshape(
        row_count, local_groups, STATE
    )
    c_all = convolved[:, chan_width + group_width :].reshape(row_count, local_groups, STATE)
    step_dt = jax.nn.softplus(dt_raw + dt_bias)
    step_rate = -step_dt * decay_rate
    seg_before = seg_ext[tail_len - 1]
    block_total = row_count // BLOCK

    def to_blocks(values):
        return values.reshape((block_total, BLOCK) + values.shape[1:])

    start_state = (jnp.zeros((head_count, HEAD_DIM, STATE), jnp.float32), seg_before)
    final, outputs = lax.scan(
        block_step,
        start_state,
        (
            to_blocks(x_all),
            to_blocks(b_all),
            to_blocks(c_all),
            to_blocks(step_dt),
            to_blocks(step_rate),
            to_blocks(segment_ids),
        ),
    )
    local_state = final[0]
    scan_out = outputs.reshape(row_count, head_count, HEAD_DIM)
    running = jnp.cumsum(step_rate, axis=0)
    carry_gain = jnp.where(segment_ids[-1] == seg_before, jnp.exp(running[-1]), 0.0)
    neutral = (jnp.ones((head_count,), jnp.float32), jnp.zeros_like(local_state))
    incoming = carried_in((carry_gain, local_state), "dp", chain_combine, neutral)[1]
    c_heads = jnp.repeat(c_all.astype(jnp.float32), head_count // local_groups, axis=1)
    entry_mask = jnp.where((segment_ids == seg_before)[:, None], jnp.exp(running), 0.0)
    scan_out = scan_out + entry_mask[:, :, None] * jnp.einsum(
        "thn,hpn->thp", c_heads, incoming, precision=highest
    )
    scan_out = scan_out + skip_gain[None, :, None] * x_all.astype(jnp.float32)
    gated_out = scan_out.reshape(row_count, chan_width) * jax.nn.silu(gate_in.astype(jnp.float32))
    grouped = gated_out.reshape(row_count, local_groups, chan_width // local_groups)
    inv_rms = lax.rsqrt(jnp.mean(grouped * grouped, axis=2, keepdims=True) + 1e-05)
    normed = ((grouped * inv_rms).reshape(row_count, chan_width) * norm_gain).astype(jnp.bfloat16)
    return lax.psum_scatter(
        lax.dot_general(
            normed, w_out, (((1,), (1,)), ((), ())), preferred_element_type=jnp.float32
        ).astype(jnp.bfloat16),
        "mp",
        scatter_dimension=0,
        tiled=True,
    )


def solution(mesh):
    placed = (
        P("dp", None),
        P("dp"),
        P("dp"),
        P("dp", "mp"),
        P("dp", "mp"),
        P(None, "mp"),
        P(None, "mp"),
        P(None, None, "mp"),
        P("mp"),
        P("mp"),
        P("mp"),
        P("mp"),
    )
    return jax.shard_map(
        on_device, mesh=mesh, in_specs=placed, out_specs=P(("dp", "mp"), None), check_vma=False
    )
```

profile of v0, /device:TPU:0, one launch (start us, length us, event | category | flops | bytes accessed | tf_op | source)
XLA Modules:
  0.0 450.1 jit_solution(5669113875666514030)
XLA Ops:
  7.6 1.4 scatter_custom_fusion
  9.1 9.6 %all_to_all.14 = s32[8,1,64]{2,1,0:T(1,128)S(1)} all-to-all(s32[8,1,64]{2,1,0:T(1,128)S(1)} %all_to_all.9), channel_id=1, replica_groups=mesh['dp'=8,'mp'=4] {'dp'}, dimensions={0} | all-to-all | bytes 4096 | tf_op jit(solution)/shard_map/all_to_all | solution.py:105
  18.8 4.4 gather_fusion
  23.2 6.0 %broadcast_select_fusion = bf16[8,64,4096]{2,1,0:T(8,128)(2,1)} fusion(bf16[8,64,4096]{2,1,0:T(8,128)(2,1)} %bitcast.118, pred[8,64]{1,0:T(8,128)(4,1)S(1)} %compare_bitcast_fusion), kind=kLoop, calls=%fused_computation.10 | loop fusion | flops 2097152 | bytes 8389120 | tf_op jit(solution)/shard_map/jit(_where)/select_n | solution.py:106
  29.2 4.7 %all-to-all-start.1 = ((bf16[8,64,4096]{2,1,0:T(8,128)(2,1)}), bf16[8,64,4096]{2,1,0:T(8,128)(2,1)}, u32[]{:S(2)}, u32[]{:S(2)}) async-start(bf16[8,64,4096]{2,1,0:T(8,128)(2,1)} %broadcast_select_fusion), calls=%async_computation.1 | async-start | bytes 8388608 | tf_op jit(solution)/shard_map/all_to_all | solution.py:109
  34.1 2.2 collective-permute-start
  36.9 95.3 %all_gather.17 = bf16[4096,32]{0,1:T(8,128)(2,1)S(1)} all-gather(bf16[512,32]{0,1:T(8,128)(2,1)S(1)} %copy-done.6), channel_id=1, replica_groups=mesh['dp'=8,'mp'=4] {'dp'}, dimensions={0}, use_global_device_ids=true | all-gather | bytes 294912 | tf_op jit(solution)/shard_map/all_gather | solution.py:118
  134.1 1.3 slice_compare_fusion.2
  135.4 7.7 %gather_fusion.1 = bf16[256,4096]{1,0:T(8,128)(2,1)S(1)} fusion(bf16[512,4096]{1,0:T(8,128)(2,1)} %bitcast.7, s32[1024]{0:T(1024)S(1)} %pad_clamp_fusion), kind=kCustom, calls=%fused_computation.1 | custom fusion | bytes 4195328 | tf_op jit(solution)/shard_map/gather | solution.py:110
  145.1 110.0 %all-gather.5.cloned.1.call-done = bf16[4096,5120]{1,0:T(8,128)(2,1)} async-done(((bf16[512,5120]{1,0:T(8,128)(2,1)}), bf16[4096,5120]{1,0:T(8,128)(2,1)}) %all-gather.5.cloned.1.call-update) | async-done | bytes 41943056 | tf_op jit(solution)/shard_map/all_gather | solution.py:115
  255.1 18.9 %convolution_convert_fusion = bf16[256,5120]{1,0:T(8,128)(2,1)} fusion(bf16[256,4096]{1,0:T(8,128)(2,1)S(1)} %gather_fusion.1, bf16[4096,5120]{1,0:T(8,128)(2,1)} %all-gather.5.cloned.1.call-done), kind=kOutput, calls=%fused_computation.8 | convolution fusion | flops 10738728960 | bytes 46661632 | tf_op jit(solution)/shard_map/dot_general | solution.py:114
  274.0 1.3 slice.104
  275.3 1.1 slice.105
  276.5 2.7 collective-permute-start.1
  280.4 2.7 multiply_convert_fusion
  283.8 0.9 broadcast_in_dim.181
  284.8 6.4 %add_convert_fusion = bf16[32,64,256]{2,1,0:T(8,128)(2,1)} fusion(f32[256,32,256]{2,0,1:T(8,128)S(1)} %bitcast.117, bf16[256,32,64]{0,2,1:T(8,128)(2,1)S(1)} %bitcast.119, f32[256,32]{0,1:T(8,128)S(1)} %get-tuple-element.97, f32[32]{0:T(128)S(1)} %fusion.30), kind=kOutput, calls=%fused_computation.27 | convolution fusion | flops 1612709888 | bytes 10518656 | tf_op jit(solution)/shard_map/while/body/eval_jaxpr/shp,shn->hpn/dot_general | solution.py:70
  291.6 11.0 %all-gather.1 = bf16[8,1,32]{2,1,0:T(2,128)(2,1)S(1)} all-gather(bf16[1,1,32]{2,1,0:T(2,128)(2,1)S(1)} %bitcast.138), channel_id=1, replica_groups=mesh['dp'=8,'mp'=4] {'dp'}, dimensions={0}, use_global_device_ids=true | all-gather | bytes 576 | tf_op jit(solution)/shard_map/all_gather | solution.py:24
  302.9 2.5 fusion.1
  305.5 2.7 fusion.37
  308.2 0.9 broadcast_in_dim.177
  309.1 3.2 copy-done.2
  312.4 9.5 %fusion.12 = f32[32,64,256]{2,1,0:T(8,128)} fusion(f32[256,32,256]{2,0,1:T(8,128)S(1)} %bitcast.115), kind=kOutput, calls=%fused_computation.35 | convolution fusion | flops 1610612736 | bytes 10485760 | tf_op jit(solution)/shard_map/while/body/eval_jaxpr/thn,hpn->thp/dot_general | solution.py:61
  321.8 26.0 %all-gather.7.cloned.1.call-done = bf16[256,64,256]{2,1,0:T(8,128)(2,1)} async-done(((bf16[32,64,256]{2,1,0:T(8,128)(2,1)}), bf16[256,64,256]{2,1,0:T(8,128)(2,1)}) %all-gather.7.cloned.1.call-update) | async-done | bytes 8388624 | tf_op jit(solution)/shard_map/all_gather | solution.py:24
  348.8 14.2 %fusion.3 = f32[256,32,64]{0,2,1:T(8,128)} fusion(bf16[256,32,64]{0,2,1:T(8,128)(2,1)S(1)} %bitcast.121, f32[32,64,256]{2,1,0:T(8,128)} %fusion.12, f32[32,64,256]{2,1,0:T(8,128)} %fusion.37, f32[32,64,256]{2,1,0:T(8,128)S(1)} %get-tuple-element.79, f32[256,32,256]{2,0,1:T(8,128)} %bitcast.116, f32[32]{0:T(128)S(1)} %copy-done.11, ...), kind=kOutput, calls=%fused_computation.17 | convolution fusion | flops 1614282752 | bytes 17858688 | tf_op jit(solution)/shard_map/thn,hpn->thp/dot_general | solution.py:177
  362.9 2.2 copy.78
  365.1 3.9 fusion.34
  369.0 4.0 mul.209
  373.0 2.2 reduce_sum.19
  375.9 0.9 copy.87
  377.8 10.2 %convolution_convert_fusion.1 = bf16[256,4096]{1,0:T(8,128)(2,1)} fusion(bf16[4096,2048]{1,0:T(8,128)(2,1)} %param.19, f32[256,2048]{1,0:T(8,128)S(1)} %bitcast.127, f32[2048]{0:T(1024)S(1)} %copy-done.14, f32[256,2048]{1,0:T(8,128)S(1)} %copy-done.4, bf16[256,5120]{1,0:T(8,128)(2,1)S(1)} %copy-done.5), kind=kOutput, calls=%fused_computation.9 | convolution fusion | flops 4300734464 | bytes 24125440 | tf_op jit(solution)/shard_map/dot_general | solution.py:186
  388.0 55.3 %reduce-scatter.2.cloned.1.call-done = bf16[64,4096]{1,0:T(8,128)(2,1)} async-done(((bf16[256,4096]{1,0:T(8,128)(2,1)}), bf16[64,4096]{1,0:T(8,128)(2,1)}) %reduce-scatter.2.cloned.1.call-update) | async-done | bytes 524304 | tf_op jit(solution)/shard_map/reduce_scatter | solution.py:185
  (84 shorter events, 9.8 us)
Async XLA Ops:
  6.5 12.3 %copy-start = (bf16[256,4096]{1,0:T(8,128)(2,1)S(1)}, bf16[256,4096]{1,0:T(8,128)(2,1)}, u32[]{:S(2)}) copy-start(bf16[256,4096]{1,0:T(8,128)(2,1)} %param.14) | copy-start | bytes 6291460
  6.5 0.8 copy-start.10
  6.5 248.6 %all-gather.5.cloned.1.call-start = ((), (), s32[]{:S(2)}) async-start(), calls=%async_computation.3 | async-start | bytes 47185920 | tf_op jit(solution)/shard_map/all_gather | solution.py:115
  29.2 4.8 %copy-start.8 = (s32[256]{0:T(256)S(1)}, s32[256]{0:T(256)}, u32[]{:S(2)}) copy-start(s32[256]{0:T(256)} %param.16) | copy-start | bytes 3076
  29.2 7.6 %copy-start.9 = (f32[4,2,512]{2,1,0:T(2,128)S(1)}, f32[4,2,512]{2,1,0:T(2,128)}, u32[]{:S(2)}) copy-start(f32[4,2,512]{2,1,0:T(2,128)} %param.21) | copy-start | bytes 49156
  29.2 7.6 %copy-start.6 = (bf16[512,32]{0,1:T(8,128)(2,1)S(1)}, bf16[512,32]{0,1:T(8,128)(2,1)}, u32[]{:S(2)}) copy-start(bf16[512,32]{0,1:T(8,128)(2,1)} %param.18) | copy-start | bytes 98308
  29.2 103.0 %copy-start.7 = (f32[4,2048]{1,0:T(4,128)S(1)}, f32[4,2048]{1,0:T(4,128)}, u32[]{:S(2)}) copy-start(f32[4,2048]{1,0:T(4,128)} %param.20) | copy-start | bytes 98308
  29.2 106.2 %all-to-all-start.1 = ((bf16[8,64,4096]{2,1,0:T(8,128)(2,1)}), bf16[8,64,4096]{2,1,0:T(8,128)(2,1)}, u32[]{:S(2)}, u32[]{:S(2)}) async-start(bf16[8,64,4096]{2,1,0:T(8,128)(2,1)} %broadcast_select_fusion), calls=%async_computation.1 | async-start | bytes 8388608 | tf_op jit(solution)/shard_map/all_to_all | solution.py:109
  33.9 313.9 %all-gather.7.cloned.1.call-start = ((), (), s32[]{:S(2)}) async-start(), calls=%async_computation.5 | async-start | bytes 9437184 | tf_op jit(solution)/shard_map/all_gather | solution.py:24
  34.1 98.2 %collective-permute-start = (f32[3]{0:T(128)S(1)}, f32[3]{0:T(128)S(1)}, u32[]{:S(2)}, u32[]{:S(2)}) collective-permute-start(f32[3]{0:T(128)S(1)} %add_convert_fusion.1), channel_id=1, source_target_pairs={{0,4},{4,8},{8,12},{12,16},{16,20},{20,24},{24,28},{1,5},{5,9},{9,... | collective-permute-start | bytes 44 | tf_op jit(solution)/shard_map/ppermute | solution.py:18
  135.4 7.7 %copy-start.13 = (f32[32]{0:T(128)S(1)}, f32[32]{0:T(128)}, u32[]{:S(2)}) copy-start(f32[32]{0:T(128)} %param.22) | copy-start | bytes 388
  143.1 0.8 copy-start.12
  276.5 3.5 collective-permute-start.1
  291.2 152.1 %reduce-scatter.2.cloned.1.call-start = ((), (), s32[]{:S(2)}) async-start(), calls=%async_computation.4 | async-start | bytes 2621440 | tf_op jit(solution)/shard_map/reduce_scatter | solution.py:185
  309.1 3.2 copy-start.2
  348.1 0.7 copy-start.11
  365.1 3.9 copy-start.3
  375.3 1.7 copy-start.5
  375.9 1.9 copy-start.4
  375.9 1.9 copy-start.14
  377.8 65.5 %copy-start.1 = (bf16[256,4096]{1,0:T(8,128)(2,1)S(1)}, bf16[256,4096]{1,0:T(8,128)(2,1)}, u32[]{:S(2)}) copy-start(bf16[256,4096]{1,0:T(8,128)(2,1)} %param.14) | copy-start | bytes 6291460
Sparse Core Ops, SparseCore 0:
  9.3 245.8 all-gather.4
  291.3 56.4 all-gather.6
  388.2 55.0 reduce-scatter.1
where the time goes:
time: 459 us; the launch traced here: 450 us
  waiting for transfers between devices  193 us (42%)
  blocking collectives  116 us (25%)
  matrix products  62.8 us (14%)
  local copies, waits for them, and re-layouts  33 us (7%)
  other arithmetic  20.6 us (4%)
  between operations  15 us (3%)
  starting transfers between devices  9.67 us (2%)
    all_gather x1, waiting for transfers between devices, on_device(): lax.all_gather(w_in, 'dp', axis=0, tiled=True)  110 us
    all_gather x1, blocking collectives, on_device(): lax.all_gather(w_dt, 'dp', axis=0, tiled=True)  95.3 us
    reduce_scatter x1, waiting for transfers between devices, on_device(): lax.psum_scatter(lax.dot_general(normed, w_out, (((1,), (1,)), ((), ())),...  55.3 us
    all_gather x1, waiting for transfers between devices, carried_in(): lax.all_gather(a.astype(kind), axis)  26 us
    dot_general x1, matrix products, on_device(): jnp.dot(gathered, lax.all_gather(w_in, 'dp', axis=0, tiled=True), preferr...  18.9 us
    dot_general x1, matrix products, on_device(): jnp.einsum('thn,hpn->thp', c_heads, incoming, precision=highest)  14.2 us
    all_gather x1, blocking collectives, carried_in(): lax.all_gather(a.astype(kind), axis)  11 us
    dot_general x1, matrix products, on_device(): lax.dot_general(normed, w_out, (((1,), (1,)), ((), ())), preferred_elemen...  10.2 us
  transfers between devices with their start and end apart: 6, of which 4 were waited for; matrix products, arithmetic and copies ran while one was open for 9% of the time, Pallas kernels for 0%

commit v1 on v0

--- a/solution.py
+++ b/solution.py
@@ -1,6 +1,8 @@
 import jax
 import jax.numpy as jnp
 from jax import lax
+from jax.experimental import pallas as pl
+from jax.experimental.pallas import tpu as pltpu
 from jax.sharding import PartitionSpec as P
 
 HEAD_DIM = 64
@@ -192,6 +194,375 @@
     )
 
 
+HALO = 16
+MESH = pl.DeviceIdType.MESH
+
+
+def remote(src, dst, send, recv, dp):
+    return pltpu.make_async_remote_copy(
+        src_ref=src, dst_ref=dst, send_sem=send, recv_sem=recv,
+        device_id={"dp": dp}, device_id_type=MESH,
+    )
+
+
+def projection_kernel(
+    tok_hbm, meta_ref, w_hbm, wdt_ref,
+    xb_out, dt_out, zc_out, meta_out,
+    tokg, metas, wbuf, idxcol, onehot, packed, own,
+    s_da, s_db, s_xa, s_yb, s_ya, s_xb,
+    r_da, r_db, r_xa, r_yb, r_sa, r_sb,
+    loc_sem, meta_send, meta_recv, w_send, w_recv,
+    tok_send, tok_recv, fwd_send, fwd_recv, red_send, red_recv,
+):
+    me = lax.axis_index("dp")
+    core = me % 2
+    chip = me // 2
+    at_x = chip % 2
+    at_y = chip // 2
+    chip_x = chip + 1 - 2 * at_x
+    chip_y = chip + 2 - 4 * at_y
+    chip_d = chip_x + chip_y - chip
+    sibling = me + 1 - 2 * core
+    rows, depth = tok_hbm.shape[0], w_hbm.shape[0]
+    width = w_hbm.shape[1] // 5
+    group, state = width, width // 4
+    kdim = 2 * depth
+    block = 2 * rows
+    na = xb_out.shape[1]
+    nb = zc_out.shape[1]
+
+    barrier = pltpu.get_barrier_semaphore()
+    for k in range(1, 8):
+        pl.semaphore_signal(barrier, inc=1, device_id={"dp": (me + k) % 8}, device_id_type=MESH)
+    pl.semaphore_wait(barrier, 7)
+
+    mine = pl.ds(pl.multiple_of(me * rows, rows), rows)
+
+    def columns(of_chip):
+        return pl.ds(pl.multiple_of(of_chip * kdim, 128), kdim)
+
+    copies = []
+    for k in range(1, 8):
+        copies.append(
+            remote(meta_ref, metas.at[me], meta_send.at[k - 1], meta_recv.at[k - 1], (me + k) % 8)
+        )
+    directs = []
+    for i, to in enumerate((chip_d, chip_x, chip_y)):
+        directs.append(
+            remote(tok_hbm.at[:, columns(to)], tokg.at[mine], tok_send.at[i], tok_recv.at[i],
+                   2 * to + core)
+        )
+    for c in copies + directs:
+        c.start()
+    local = [
+        pltpu.make_async_copy(tok_hbm.at[:, columns(chip)], tokg.at[mine], loc_sem.at[0]),
+        pltpu.make_async_copy(meta_ref, metas.at[me], loc_sem.at[1]),
+    ]
+    forward = [
+        remote(tok_hbm.at[:, columns(chip)], tokg.at[mine], fwd_send.at[0], fwd_recv.at[0], sibling)
+    ]
+    kmine = pl.ds(pl.multiple_of(core * depth, depth), depth)
+
+    def pieces(g):
+        return (
+            (w_hbm.at[:, pl.ds(pl.multiple_of(g * group, 128), group)], 0, group),
+            (w_hbm.at[:, pl.ds(pl.multiple_of(4 * group + g * state, 128), state)], group, state),
+            (wdt_ref.at[g], na, 128),
+            (w_hbm.at[:, pl.ds(pl.multiple_of(2 * group + g * group, 128), group)], na + 128, group),
+            (w_hbm.at[:, pl.ds(pl.multiple_of(4 * group + 2 * state + g * state, 128), state)],
+             na + 128 + group, state),
+        )
+
+    weights = []
+    for i, (src, col, size) in enumerate(pieces(1 - core)):
+        weights.append(
+            remote(src, wbuf.at[kmine, pl.ds(col, size)], w_send.at[i], w_recv.at[i], sibling)
+        )
+    for i, (src, col, size) in enumerate(pieces(core)):
+        local.append(
+            pltpu.make_async_copy(src, wbuf.at[kmine, pl.ds(col, size)], loc_sem.at[2 + i])
+        )
+    for c in forward + weights + local:
+        c.start()
+
+    for c in copies:
+        c.wait_recv()
+    local[1].wait()
+    idxcol[0:HALO, :] = jnp.full((HALO, 128), -1, jnp.int32)
+    for j in range(8):
+        row = metas[j, 0:1, :]
+        idxcol[HALO + j * rows : HALO + (j + 1) * rows, :] = jnp.broadcast_to(row, (128, rows)).T
+    meta_out[...] = metas[...]
+
+    for i, source in enumerate((chip_d, chip_x, chip_y)):
+        directs[i].wait_recv()
+        theirs = pl.ds(pl.multiple_of((2 * source + core) * rows, rows), rows)
+        c = remote(tokg.at[theirs], tokg.at[theirs], fwd_send.at[1 + i], fwd_recv.at[1 + i], sibling)
+        c.start()
+        forward.append(c)
+    for c in local[:1] + local[2:]:
+        c.wait()
+    for c in weights + forward:
+        c.wait_recv()
+
+    lanes = lax.broadcasted_iota(jnp.int32, (block + HALO, 128), 1)
+
+    def pack(of_chip, slot):
+        ids = idxcol[pl.ds(pl.multiple_of(of_chip * block, block), block + HALO), :]
+
+        @pl.loop(0, 8 * rows // 128)
+        def _(t):
+            onehot[:, pl.ds(pl.multiple_of(t * 128, 128), 128)] = jnp.where(
+                ids == lanes + t * 128, 1.0, 0.0
+            ).astype(jnp.bfloat16)
+
+        @pl.loop(0, kdim // 256)
+        def _(t):
+            cols = pl.ds(pl.multiple_of(t * 256, 256), 256)
+            packed[slot, :, cols] = jnp.dot(
+                onehot[...], tokg[:, cols], preferred_element_type=jnp.float32
+            ).astype(jnp.bfloat16)
+
+    def product(slot, col, size):
+        return jnp.dot(
+            packed[slot], wbuf[:, pl.ds(col, size)], preferred_element_type=jnp.float32
+        )
+
+    def split(acc):
+        high = acc.astype(jnp.bfloat16).astype(jnp.float32)
+        return jnp.where(lanes < 16, high, acc - high).astype(jnp.bfloat16)
+
+    def joined(ref):
+        r = ref[:, na : na + 128].astype(jnp.float32)
+        return r + jnp.where(lanes < 16, pltpu.roll(r, 112, 1), pltpu.roll(r, 16, 1))
+
+    def part_a(slot, out, add=None):
+        @pl.loop(0, na // 256)
+        def _(t):
+            col = pl.multiple_of(t * 256, 256)
+            acc = product(slot, col, 256)
+            if add is not None:
+                acc = acc + add[:, pl.ds(col, 256)].astype(jnp.float32)
+            out[:, pl.ds(col, 256)] = acc.astype(jnp.bfloat16)
+
+        acc = product(slot, na, 128)
+        if add is not None:
+            acc = acc + joined(add)
+        out[:, na : na + 128] = split(acc)
+
+    def part_b(slot, out, add=None):
+        @pl.loop(0, nb // 256)
+        def _(t):
+            col = pl.multiple_of(t * 256, 256)
+            acc = product(slot, pl.multiple_of(na + 128 + col, 128), 256)
+            if add is not None:
+                acc = acc + add[:, pl.ds(col, 256)].astype(jnp.float32)
+            out[:, pl.ds(col, 256)] = acc.astype(jnp.bfloat16)
+
+    dev_x, dev_y = 2 * chip_x + core, 2 * chip_y + core
+    c_da = remote(s_da, r_da, red_send.at[0], red_recv.at[0], dev_x)
+    c_db = remote(s_db, r_db, red_send.at[1], red_recv.at[1], dev_y)
+    c_xa = remote(s_xa, r_xa, red_send.at[2], red_recv.at[2], dev_x)
+    c_yb = remote(s_yb, r_yb, red_send.at[3], red_recv.at[3], dev_y)
+    c_ya = remote(s_ya, r_sa, red_send.at[4], red_recv.at[4], dev_y)
+    c_xb = remote(s_xb, r_sb, red_send.at[5], red_recv.at[5], dev_x)
+    pack(chip_d, 0)
+    part_a(0, s_da)
+    c_da.start()
+    part_b(0, s_db)
+    c_db.start()
+    pack(chip_x, 1)
+    part_a(1, s_xa)
+    c_xa.start()
+    pack(chip_y, 2)
+    part_b(2, s_yb)
+    c_yb.start()
+    pack(chip, 0)
+
+    @pl.loop(0, na // 256)
+    def _(t):
+        col = pl.multiple_of(t * 256, 256)
+        own[:, pl.ds(col, 256)] = product(0, col, 256)
+
+    own[:, na : na + 128] = product(0, na, 128)
+
+    @pl.loop(0, nb // 256)
+    def _(t):
+        col = pl.multiple_of(na + 128 + t * 256, 128)
+        own[:, pl.ds(col, 256)] = product(0, col, 256)
+
+    c_da.wait_recv()
+    part_a(2, s_ya, r_da)
+    c_ya.start()
+    c_db.wait_recv()
+    part_b(1, s_xb, r_db)
+    c_xb.start()
+    c_xa.wait_recv()
+    c_yb.wait_recv()
+    c_ya.wait_recv()
+
+    @pl.loop(0, na // 256)
+    def _(t):
+        cols = pl.ds(pl.multiple_of(t * 256, 256), 256)
+        xb_out[:, cols] = (
+            own[:, cols] + r_xa[:, cols].astype(jnp.float32) + r_sa[:, cols].astype(jnp.float32)
+        ).astype(jnp.bfloat16)
+
+    dt_out[...] = own[:, na : na + 128] + joined(r_xa) + joined(r_sa)
+    c_xb.wait_recv()
+
+    @pl.loop(0, nb // 256)
+    def _(t):
+        cols = pl.ds(pl.multiple_of(t * 256, 256), 256)
+        own_cols = pl.ds(pl.multiple_of(na + 128 + t * 256, 128), 256)
+        zc_out[:, cols] = (
+            own[:, own_cols] + r_yb[:, cols].astype(jnp.float32) + r_sb[:, cols].astype(jnp.float32)
+        ).astype(jnp.bfloat16)
+
+    for c in copies + directs + forward + weights + [c_da, c_db, c_xa, c_yb, c_ya, c_xb]:
+        c.wait_send()
+
+
+def project(tokens, meta, w_in, wdt):
+    rows, depth = tokens.shape[0], w_in.shape[0]
+    width = w_in.shape[1] // 5
+    na = width + width // 4
+    nb = na
+    m = 2 * rows + HALO
+    bf = jnp.bfloat16
+    vmem = pl.BlockSpec(memory_space=pltpu.VMEM)
+    hbm = pl.BlockSpec(memory_space=pl.ANY)
+    dma = pltpu.SemaphoreType.DMA
+    a, b = pltpu.VMEM((m, na + 128), bf), pltpu.VMEM((m, nb), bf)
+    return pl.pallas_call(
+        projection_kernel,
+        out_shape=(
+            jax.ShapeDtypeStruct((m, na), bf),
+            jax.ShapeDtypeStruct((m, 128), jnp.float32),
+            jax.ShapeDtypeStruct((m, nb), bf),
+            jax.ShapeDtypeStruct((8, 8, rows), jnp.int32),
+        ),
+        in_specs=[hbm, vmem, hbm, vmem],
+        out_specs=(vmem,) * 4,
+        scratch_shapes=[
+            pltpu.VMEM((8 * rows, 2 * depth), bf),
+            pltpu.VMEM((8, 8, rows), jnp.int32),
+            pltpu.VMEM((2 * depth, na + 128 + nb), bf),
+            pltpu.VMEM((8 * rows + HALO, 128), jnp.int32),
+            pltpu.VMEM((m, 8 * rows), bf),
+            pltpu.VMEM((3, m, 2 * depth), bf),
+            pltpu.VMEM((m, na + 128 + nb), jnp.float32),
+            a, b, a, b, a, b,
+            a, b, a, b, a, b,
+            dma((7,)), dma((7,)), dma((7,)), dma((5,)), dma((5,)),
+            dma((3,)), dma((3,)), dma((4,)), dma((4,)), dma((6,)), dma((6,)),
+        ],
+        compiler_params=pltpu.CompilerParams(
+            collective_id=0, has_side_effects=True, vmem_limit_bytes=58 << 20
+        ),
+    )(tokens, meta, w_in, wdt)
+
+
+def on_plane(
+    tokens, pack_source, segment_ids, w_in, w_dt, w_out, conv_x, conv_bc,
+    dt_bias, decay_rate, skip_gain, norm_gain,
+):
+    f32, bf = jnp.float32, jnp.bfloat16
+    rows = tokens.shape[0]
+    total = 8 * rows
+    block = 2 * rows
+    me = lax.axis_index("dp")
+    core, chip = me % 2, me // 2
+    heads = w_dt.shape[1] // 2
+    chans = w_out.shape[1] // 2
+
+    def mine(values, axis):
+        size = values.shape[axis] // 2
+        return lax.dynamic_slice_in_dim(values, core * size, size, axis)
+
+    meta = jnp.pad(jnp.stack([pack_source, segment_ids]), ((0, 6), (0, 0)))
+    halves = w_dt.reshape(w_dt.shape[0], 2, heads).transpose(1, 0, 2)
+    wdt = jnp.pad(jnp.concatenate([halves, halves], axis=2), ((0, 0), (0, 0), (0, 128 - 2 * heads)))
+    xb, dt_raw, zc, metas = project(tokens, meta, w_in, wdt)
+    seg_all = jnp.concatenate([jnp.full((HALO,), -1, jnp.int32), metas[:, 1, :].reshape(total)])
+    seg_ext = lax.dynamic_slice_in_dim(seg_all, chip * block, block + HALO, 0)
+    seg = seg_ext[HALO:]
+    seg_before = seg_ext[HALO - 1]
+    taps_bc = mine(conv_bc, 2)
+
+    def convolve(values, taps):
+        total_sum = jnp.zeros((block, values.shape[1]), f32)
+        for lag in range(CONV):
+            first = HALO - CONV + 1 + lag
+            same = (seg_ext[first : first + block] == seg)[:, None]
+            total_sum = total_sum + jnp.where(
+                same, taps[lag][None, :] * values[first : first + block].astype(f32), 0.0
+            )
+        return jax.nn.silu(total_sum).astype(bf)
+
+    x = convolve(xb[:, :chans], mine(conv_x, 1))
+    b = convolve(xb[:, chans:], taps_bc[:, 0])
+    c = convolve(zc[:, chans:], taps_bc[:, 1])
+    gate = jax.nn.silu(zc[HALO:, :chans].astype(f32))
+    step_dt = jax.nn.softplus(dt_raw[HALO:, :heads] + mine(dt_bias, 0))
+    step_rate = -step_dt * mine(decay_rate, 0)
+    places = jnp.arange(block)
+    lower = (places[:, None] >= places[None, :])
+    cum = jnp.dot(lower.astype(f32), step_rate, precision=highest)
+    xh = x.reshape(block, heads, HEAD_DIM)
+
+    last = seg[-1]
+    weight = jnp.where((seg == last)[:, None], jnp.exp(cum[-1][None, :] - cum), 0.0) * step_dt
+    wide = jnp.repeat(weight, HEAD_DIM, axis=1)
+    weighted = (wide * x.astype(f32)).astype(bf)
+    left = lax.dot_general(weighted, b, (((0,), (0,)), ((), ())), preferred_element_type=f32)
+    gain = jnp.where(last == seg_before, jnp.exp(cum[-1]), 0.0)
+    sent = jnp.concatenate(
+        [left.reshape(heads, HEAD_DIM * STATE), jnp.broadcast_to(gain[:, None], (heads, 128))], axis=1
+    ).astype(bf)
+    groups = [[i, i + 2, i + 4, i + 6] for i in range(2)]
+    gathered = lax.all_gather(sent, "dp", axis_index_groups=groups).astype(f32)
+
+    linked = (seg[:, None] == seg[None, :]) & lower
+    cum_t = cum.T
+    spans = cum_t[:, :, None] - cum_t[:, None, :]
+    decay = jnp.where(linked[None], jnp.exp(jnp.where(linked[None], spans, 0.0)), 0.0)
+    scores = lax.dot_general(c, b, (((1,), (1,)), ((), ())), preferred_element_type=f32)
+    mixing = (scores[None] * decay * step_dt.T[:, None, :]).astype(bf)
+    ssd = jnp.einsum("hts,shp->thp", mixing, xh, preferred_element_type=f32).reshape(block, chans)
+
+    incoming = jnp.zeros((heads, HEAD_DIM * STATE), f32)
+    for k in range(3):
+        part = gathered[k]
+        incoming = jnp.where(
+            k < chip, part[:, -1:] * incoming + part[:, : HEAD_DIM * STATE], incoming
+        )
+    before = incoming.reshape(chans, STATE).astype(bf)
+    entry = jnp.where((seg == seg_before)[:, None], jnp.exp(cum), 0.0)
+    ssd = ssd + jnp.repeat(entry, HEAD_DIM, axis=1) * lax.dot_general(
+        c, before, (((1,), (1,)), ((), ())), preferred_element_type=f32
+    )
+    skip = jnp.repeat(mine(skip_gain, 0), HEAD_DIM)[None, :]
+    gated = (ssd + skip * x.astype(f32)) * gate
+    inv = lax.rsqrt(jnp.mean(gated * gated, axis=1, keepdims=True) + 1e-05)
+    normed = (gated * inv * mine(norm_gain, 0)[None, :]).astype(bf)
+
+    keep = lax.dynamic_slice_in_dim(normed, core * rows, rows, 0)
+    give = lax.dynamic_slice_in_dim(normed, (1 - core) * rows, rows, 0)
+    got = lax.ppermute(give, "dp", [(i, i + 1 - 2 * (i % 2)) for i in range(8)])
+    whole = jnp.where(
+        core == 0, jnp.concatenate([keep, got], axis=1), jnp.concatenate([got, keep], axis=1)
+    )
+    return lax.psum_scatter(
+        lax.dot_general(
+            whole, w_out, (((1,), (1,)), ((), ())), preferred_element_type=f32
+        ).astype(bf),
+        "mp",
+        scatter_dimension=0,
+        tiled=True,
+    )
+
+
 def solution(mesh):
     placed = (
         P("dp", None),
@@ -207,6 +578,7 @@
         P("mp"),
         P("mp"),
     )
+    body = on_plane if mesh.shape["dp"] == 8 else on_device
     return jax.shard_map(
-        on_device, mesh=mesh, in_specs=placed, out_specs=P(("dp", "mp"), None), check_vma=False
-    )
+        body, mesh=mesh, in_specs=placed, out_specs=P(("dp", "mp"), None), check_vma=False
+    )

time: 459 us -> 278 us (0.61)
  the two profiles are of different devices: /device:TPU:0 before, /device:TPU:20 now
where the time goes in v1:
time: 278 us; the launch traced here: 275 us
  Pallas kernels  134 us (48%)
  waiting for transfers between devices  65.9 us (24%)
  matrix products  31 us (11%)
  local copies, waits for them, and re-layouts  17.4 us (6%)
  between operations  15 us (5%)
  other arithmetic  11.9 us (4%)
    pallas_call x1, Pallas kernels, project(): pl.pallas_call(projection_kernel, out_shape=(jax.ShapeDtypeStruct((m, na)...  134 us
    reduce_scatter x1, waiting for transfers between devices, on_plane(): lax.psum_scatter(lax.dot_general(whole, w_out, (((1,), (1,)), ((), ())),...  43.4 us
    all_gather x1, waiting for transfers between devices, on_plane(): gathered = lax.all_gather(sent, 'dp', axis_index_groups=groups).astype(f32)  20.6 us
    dot_general x1, matrix products, on_plane(): lax.dot_general(whole, w_out, (((1,), (1,)), ((), ())), preferred_element...  18.1 us
    dot_general x1, matrix products, on_plane(): jnp.einsum('hts,shp->thp', mixing, xh, preferred_element_type=f32)  6.52 us
  transfers between devices with their start and end apart: 3, of which 3 were waited for; matrix products, arithmetic and copies ran while one was open for 6% of the time, Pallas kernels for 0%

profile of v1, /device:TPU:20, one launch (start us, length us, event | category | flops | bytes accessed | tf_op | source)
XLA Modules:
  0.0 275.2 jit_solution(4548787544044495097)
XLA Ops:
  6.5 0.7 dynamic_slice.30
  7.3 0.7 dynamic_slice.31
  8.0 0.8 pad_maximum_fusion.1
  9.0 0.7 pad_add_fusion
  9.7 0.6 pad.9.meta_ref
  10.3 0.8 pad.10.wdt_ref
  11.1 133.7 %shard_map.118 = (bf16[528,1280]{1,0:T(8,128)(2,1)}, f32[528,128]{1,0:T(8,128)}, bf16[528,1280]{1,0:T(8,128)(2,1)}, s32[8,8,256]{2,1,0:T(8,128)}) custom-call(bf16[256,4096]{1,0:T(8,128)(2,1)} %tok_hbm.1, s32[8,256]{1,0:T(8,128)} %pad.9.meta_ref, bf16[512,5120]{1,0:T(8,128)(2,1)} %w_hbm.1, bf16[2,512,128]{2,1,0:T(8,128)(2,1)} %pad.10.wdt_ref), custom_call_target="tpu_custom_call" | custom-call | tf_op jit(solution)/shard_map/pallas_call | solution.py:437
  144.7 1.6 fusion.18
  146.7 0.8 slice.173
  147.6 0.7 fusion.29
  148.2 1.4 broadcast_compare_fusion
  151.0 2.0 select_multiply_fusion
  153.0 0.3 broadcast_in_dim.169
  153.3 1.9 copy.57
  155.4 2.1 multiply_convert_fusion.3
  157.5 1.2 multiply_convert_fusion.4
  158.7 0.4 copy-done.1
  159.1 0.7 convolution_convert_fusion.1
  160.1 0.8 pad_maximum_fusion
  161.2 0.5 copy.50
  162.2 0.3 fusion.30
  162.5 6.5 %fusion = f32[16,64,512]{2,1,0:T(8,128)} fusion(bf16[512,16,64]{0,2,1:T(8,128)(2,1)S(1)} %bitcast.45, f32[16,512]{1,0:T(8,128)S(1)} %copy.52, f32[16,512]{1,0:T(8,128)S(1)} %bitcast.46, f32[512,512]{1,0:T(8,128)S(1)} %fusion.30, pred[512,512]{1,0:T(8,128)(4,1)S(1)} %fusion.19), kind=kOutput, calls=%fused_computation.1 | convolution fusion | flops 562036736 | bytes 4521984 | tf_op jit(solution)/shard_map/hts,shp->thp/dot_general | solution.py:532
  169.0 3.1 %copy.59 = f32[512,1024]{1,0:T(8,128)} copy(f32[512,1024]{0,1:T(8,128)} %bitcast.44) | data formatting | bytes 4194304 | tf_op jit(solution)/shard_map/reshape | solution.py:532
  172.2 1.6 broadcast_in_dim.167
  173.8 2.9 %copy.58 = f32[512,1024]{1,0:T(8,128)} copy(f32[512,1024]{0,1:T(8,128)} %bitcast.43) | data formatting | bytes 4194304 | tf_op jit(solution)/shard_map/reshape | solution.py:542
  176.9 20.6 %all-gather.2.cloned.1.call-done = bf16[4,16,16512]{2,1,0:T(8,128)(2,1)} async-done(((bf16[1,16,16512]{2,1,0:T(8,128)(2,1)}), bf16[4,16,16512]{2,1,0:T(8,128)(2,1)}) %all-gather.2.cloned.1.call-update) | async-done | bytes 2113552 | tf_op jit(solution)/shard_map/all_gather | solution.py:524
  197.6 1.9 convert_element_type.102
  200.0 0.4 fusion.10
  200.7 3.8 %multiply_reduce_fusion = (f32[512]{0:T(512)S(1)}, f32[512,1024]{1,0:T(8,128)S(1)}) fusion(bf16[528,1280]{1,0:T(8,128)(2,1)} %get-tuple-element.11, bf16[512,1024]{1,0:T(8,128)(2,1)S(1)} %multiply_convert_fusion.3, f32[1024]{0:T(1024)S(1)} %mul.311, f32[512,1024]{1,0:T(8,128)} %copy.59, f32[512,1024]{1,0:T(8,128)} %copy.58, ...), kind=kOutput, calls=%fused_computation.15 | convolution fusion | flops 275250688 | bytes 9181184 | tf_op jit(solution)/shard_map/dot_general | solution.py:542
  204.9 1.9 collective-permute-done
  206.8 18.1 %convolution_convert_fusion = bf16[256,4096]{1,0:T(8,128)(2,1)} fusion(bf16[4096,2048]{1,0:T(8,128)(2,1)} %param.17, bf16[256,1024]{1,0:T(8,128)(2,1)S(1)} %collective-permute-done, bf16[256,1024]{1,0:T(8,128)(2,1)S(1)} %get-tuple-element.16, pred[]{:T(512)S(6)} %eq.55), kind=kOutput, calls=%fused_computation.3 | convolution fusion | flops 4300734464 | bytes 19922944 | tf_op jit(solution)/shard_map/dot_general | solution.py:557
  225.0 43.4 %reduce-scatter.2.cloned.1.call-done = bf16[64,4096]{1,0:T(8,128)(2,1)} async-done(((bf16[256,4096]{1,0:T(8,128)(2,1)}), bf16[64,4096]{1,0:T(8,128)(2,1)}) %reduce-scatter.2.cloned.1.call-update) | async-done | bytes 524304 | tf_op jit(solution)/shard_map/reduce_scatter | solution.py:556
  (46 shorter events, 3.4 us)
Async XLA Ops:
  6.5 191.0 %all-gather.2.cloned.1.call-start = ((), (), s32[]{:S(2)}) async-start(), calls=%async_computation.1 | async-start | bytes 2641920 | tf_op jit(solution)/shard_map/all_gather | solution.py:524
  153.3 1.9 copy-start.6
  153.3 2.0 copy-start.5
  153.3 2.1 copy-start
  155.4 2.1 copy-start.4
  157.5 1.6 copy-start.1
  160.0 1.8 copy-start.3
  161.0 107.3 %reduce-scatter.2.cloned.1.call-start = ((), (), s32[]{:S(2)}) async-start(), calls=%async_computation.2 | async-start | bytes 2621440 | tf_op jit(solution)/shard_map/reduce_scatter | solution.py:556
  169.0 3.1 %copy-start.2 = (f32[512,16]{1,0:T(8,128)S(1)}, f32[512,16]{1,0:T(8,128)}, u32[]{:S(2)}) copy-start(f32[512,16]{1,0:T(8,128)} %get-tuple-element.20) | copy-start | bytes 98308
  173.8 2.9 %copy-start.7 = (f32[32]{0:T(128)S(1)}, f32[32]{0:T(128)}, u32[]{:S(2)}) copy-start(f32[32]{0:T(128)} %param.22) | copy-start | bytes 388
  200.7 3.8 %dynamic-slice-start = ((f32[2048]{0:T(1024)}, s32[]{:T(128)}), f32[1024]{0:T(1024)S(1)}, s32[]{:S(2)}) async-start(f32[2048]{0:T(1024)} %param.23, s32[]{:T(128)} %select_n.124), calls=%async_computation.3 | async-start | bytes 8704 | tf_op jit(solution)/shard_map/dynamic_slice | solution.py:481
  204.8 2.0 collective-permute-start
Sparse Core Ops, SparseCore 0:
  161.1 36.4 all-gather.1
  225.1 43.1 reduce-scatter.1

commit v2 on v1

--- a/solution.py
+++ b/solution.py
@@ -463,6 +463,141 @@
     )(tokens, meta, w_in, wdt)
 
 
+TILES = 4
+
+
+def output_kernel(normed_ref, w_hbm, out_ref, whole, wbuf, own, sent, got,
+                  loc_sem, sib_send, sib_recv, send_sem, recv_sem):
+    dp, m = lax.axis_index("dp"), lax.axis_index("mp")
+    core = dp % 2
+    sibling = dp + 1 - 2 * core
+    half = normed_ref.shape[0] // 2
+    chans = normed_ref.shape[1]
+    part = half // 4
+    step = w_hbm.shape[0] // TILES
+
+    barrier = pltpu.get_barrier_semaphore()
+    pl.semaphore_signal(barrier, inc=1, device_id={"dp": sibling}, device_id_type=MESH)
+    for k in range(1, 4):
+        pl.semaphore_signal(barrier, inc=1, device_id={"mp": (m + k) % 4}, device_id_type=MESH)
+    loads = []
+    for t in range(TILES):
+        rows = pl.ds(t * step, step)
+        loads.append(pltpu.make_async_copy(w_hbm.at[rows], wbuf.at[rows], loc_sem.at[t]))
+        loads[t].start()
+    pl.semaphore_wait(barrier, 4)
+    cols = pl.ds(pl.multiple_of(core * chans, chans), chans)
+    swap = remote(
+        normed_ref.at[pl.ds(pl.multiple_of((1 - core) * half, half), half)],
+        whole.at[:, cols], sib_send, sib_recv, sibling,
+    )
+    swap.start()
+    whole[:, cols] = normed_ref[pl.ds(pl.multiple_of(core * half, half), half), :]
+    swap.wait_recv()
+
+    inner = m * (3 - m) // 2
+    end = inner * 3 * (m - 1) + (1 - inner) * m
+    near = 1 + end // 3
+    far = 3 - near
+    opp = 3 - end
+
+    def block(j):
+        return pl.ds(pl.multiple_of(j * part, part), part)
+
+    def hop(i, slot, to, t):
+        c = pl.ds(t * step, step)
+        return pltpu.make_async_remote_copy(
+            src_ref=sent.at[i, :, c], dst_ref=got.at[slot, :, c],
+            send_sem=send_sem.at[i, t], recv_sem=recv_sem.at[slot, t],
+            device_id={"mp": to}, device_id_type=MESH,
+        )
+
+    for t in range(TILES):
+        loads[t].wait()
+
+        @pl.loop(0, step // 256)
+        def _(u):
+            c = pl.ds(pl.multiple_of(t * step + u * 256, 256), 256)
+            own[:, c] = lax.dot_general(
+                whole[...], wbuf[c, :], (((1,), (1,)), ((), ())),
+                preferred_element_type=jnp.float32,
+            )
+
+        c = pl.ds(t * step, step)
+
+        @pl.when(inner == 0)
+        def _():
+            for slot, j in ((2, opp), (1, far), (0, near)):
+                sent[slot, :, c] = own[block(j), c].astype(jnp.bfloat16)
+                hop(slot, slot, near, t).start()
+
+        @pl.when(inner == 1)
+        def _():
+            sent[0, :, c] = own[block(end), c].astype(jnp.bfloat16)
+            hop(0, 0, end, t).start()
+
+    @pl.when(inner == 1)
+    def _():
+        for t in range(TILES):
+            c = pl.ds(t * step, step)
+            for i, slot, j in ((1, 1, opp), (2, 3, far)):
+                held = 2 if i == 1 else 1
+                hop(i, held, j, t).wait_recv()
+                sent[i, :, c] = (
+                    own[block(j), c] + got[held, :, c].astype(jnp.float32)
+                ).astype(jnp.bfloat16)
+                hop(i, slot, j, t).start()
+        for t in range(TILES):
+            c = pl.ds(t * step, step)
+            hop(0, 0, end, t).wait_recv()
+            hop(0, 3, end, t).wait_recv()
+            out_ref[:, c] = (
+                own[block(m), c] + got[0, :, c].astype(jnp.float32)
+                + got[3, :, c].astype(jnp.float32)
+            ).astype(jnp.bfloat16)
+
+    @pl.when(inner == 0)
+    def _():
+        for t in range(TILES):
+            c = pl.ds(t * step, step)
+            hop(0, 0, near, t).wait_recv()
+            hop(0, 1, near, t).wait_recv()
+            out_ref[:, c] = (
+                own[block(m), c] + got[0, :, c].astype(jnp.float32)
+                + got[1, :, c].astype(jnp.float32)
+            ).astype(jnp.bfloat16)
+
+    for t in range(TILES):
+        for i in range(3):
+            hop(i, 0, near * (1 - inner) + end * inner, t).wait_send()
+    swap.wait_send()
+
+
+def project_out(normed, w_out):
+    half, chans = normed.shape[0] // 2, normed.shape[1]
+    feats = w_out.shape[0]
+    bf = jnp.bfloat16
+    vmem = pl.BlockSpec(memory_space=pltpu.VMEM)
+    dma = pltpu.SemaphoreType.DMA
+    return pl.pallas_call(
+        output_kernel,
+        out_shape=jax.ShapeDtypeStruct((half // 4, feats), bf),
+        in_specs=[vmem, pl.BlockSpec(memory_space=pl.ANY)],
+        out_specs=vmem,
+        scratch_shapes=[
+            pltpu.VMEM((half, 2 * chans), bf),
+            pltpu.VMEM((feats, 2 * chans), bf),
+            pltpu.VMEM((half, feats), jnp.float32),
+            pltpu.VMEM((3, half // 4, feats), bf),
+            pltpu.VMEM((4, half // 4, feats), bf),
+            dma((TILES,)), dma, dma, dma((3, TILES)), dma((4, TILES)),
+        ],
+        compiler_params=pltpu.CompilerParams(
+            collective_id=1, has_side_effects=True, vmem_limit_bytes=48 << 20
+        ),
+    )(normed, w_out)
+
+
 def on_plane(
     tokens, pack_source, segment_ids, w_in, w_dt, w_out, conv_x, conv_bc,
     dt_bias, decay_rate, skip_gain, norm_gain,
@@ -547,20 +682,7 @@
     inv = lax.rsqrt(jnp.mean(gated * gated, axis=1, keepdims=True) + 1e-05)
     normed = (gated * inv * mine(norm_gain, 0)[None, :]).astype(bf)
 
-    keep = lax.dynamic_slice_in_dim(normed, core * rows, rows, 0)
-    give = lax.dynamic_slice_in_dim(normed, (1 - core) * rows, rows, 0)
-    got = lax.ppermute(give, "dp", [(i, i + 1 - 2 * (i % 2)) for i in range(8)])
-    whole = jnp.where(
-        core == 0, jnp.concatenate([keep, got], axis=1), jnp.concatenate([got, keep], axis=1)
-    )
-    return lax.psum_scatter(
-        lax.dot_general(
-            whole, w_out, (((1,), (1,)), ((), ())), preferred_element_type=f32
-        ).astype(bf),
-        "mp",
-        scatter_dimension=0,
-        tiled=True,
-    )
+    return project_out(normed, w_out)
 
 
 def solution(mesh):
@@ -578,7 +700,7 @@
         P("mp"),
         P("mp"),
     )
-    body = on_plane if mesh.shape["dp"] == 8 else on_device
+    body = on_plane if mesh.shape["dp"] == 8 and mesh.shape["mp"] == 4 else on_device
     return jax.shard_map(
         body, mesh=mesh, in_specs=placed, out_specs=P(("dp", "mp"), None), check_vma=False
     )

time: 278 us -> 257 us (0.924)
  waiting for transfers between devices: 65.9 us -> 20.7 us
  Pallas kernels: 134 us -> 178 us
  matrix products: 31 us -> 13.1 us
    pallas_call x0 -> x1, Pallas kernels: none -> 44.2 us  [project_out(): pl.pallas_call(output_kernel, out_shape=jax.ShapeDtypeStruct((half // 4,...]
    reduce_scatter x1 -> x0, waiting for transfers between devices: 43.4 us -> none  [on_plane(): lax.psum_scatter(lax.dot_general(whole, w_out, (((1,), (1,)), ((), ())),...]
    dot_general x1 -> x0, matrix products: 18.1 us -> none  [on_plane(): lax.dot_general(whole, w_out, (((1,), (1,)), ((), ())), preferred_element...]
  transfers between devices with their start and end apart: 3 -> 1, of which waited for: 3 -> 1; matrix products, arithmetic and copies ran while one was open for 6% -> 6% of each run, Pallas kernels for 0% -> 0%
where the time goes in v2:
time: 257 us
  Pallas kernels  178 us (69%)
  waiting for transfers between devices  20.7 us (8%)
  local copies, waits for them, and re-layouts  18.1 us (7%)
  between operations  15 us (6%)
  matrix products  13.1 us (5%)
  other arithmetic  12 us (5%)
    pallas_call x1, Pallas kernels, project(): pl.pallas_call(projection_kernel, out_shape=(jax.ShapeDtypeStruct((m, na)...  134 us
    pallas_call x1, Pallas kernels, project_out(): pl.pallas_call(output_kernel, out_shape=jax.ShapeDtypeStruct((half // 4,...  44.2 us
    all_gather x1, waiting for transfers between devices, on_plane(): gathered = lax.all_gather(sent, 'dp', axis_index_groups=groups).astype(f32)  20.7 us
    dot_general x1, matrix products, on_plane(): jnp.einsum('hts,shp->thp', mixing, xh, preferred_element_type=f32)  6.71 us
  transfers between devices with their start and end apart: 1, of which 1 were waited for; matrix products, arithmetic and copies ran while one was open for 6% of the time, Pallas kernels for 0%

profile of v2, /device:TPU:20, one launch (start us, length us, event | category | flops | bytes accessed | tf_op | source)
XLA Modules:
  0.0 256.7 jit_solution(10898549568619422300)
XLA Ops:
  6.5 0.7 dynamic_slice.24
  7.3 0.7 dynamic_slice.25
  8.0 0.8 pad_maximum_fusion.1
  9.0 0.7 pad_add_fusion
  9.7 0.6 pad.9.meta_ref
  10.3 0.8 pad.10.wdt_ref
  11.1 133.7 %shard_map.118 = (bf16[528,1280]{1,0:T(8,128)(2,1)}, f32[528,128]{1,0:T(8,128)}, bf16[528,1280]{1,0:T(8,128)(2,1)}, s32[8,8,256]{2,1,0:T(8,128)}) custom-call(bf16[256,4096]{1,0:T(8,128)(2,1)} %tok_hbm.1, s32[8,256]{1,0:T(8,128)} %pad.9.meta_ref, bf16[512,5120]{1,0:T(8,128)(2,1)} %w_hbm.2, bf16[2,512,128]{2,1,0:T(8,128)(2,1)} %pad.10.wdt_ref), custom_call_target="tpu_custom_call" | custom-call | tf_op jit(solution)/shard_map/pallas_call | solution.py:437
  144.7 1.6 fusion.13
  146.7 0.8 slice.173
  147.6 0.7 fusion.22
  148.3 1.4 broadcast_compare_fusion
  151.0 2.0 select_multiply_fusion
  153.1 0.3 broadcast_in_dim.169
  153.4 1.9 copy.57
  155.5 2.1 multiply_convert_fusion.3
  157.6 1.2 multiply_convert_fusion.4
  158.8 0.4 copy-done.1
  159.2 0.7 convolution_convert_fusion
  160.2 0.8 pad_maximum_fusion
  161.0 0.5 copy.50
  162.0 0.3 fusion.23
  162.3 6.7 %fusion = f32[16,64,512]{2,1,0:T(8,128)} fusion(bf16[512,16,64]{0,2,1:T(8,128)(2,1)S(1)} %bitcast.44, f32[16,512]{1,0:T(8,128)S(1)} %copy.52, f32[16,512]{1,0:T(8,128)S(1)} %bitcast.45, f32[512,512]{1,0:T(8,128)S(1)} %fusion.23, pred[512,512]{1,0:T(8,128)(4,1)S(1)} %fusion.14), kind=kOutput, calls=%fused_computation.1 | convolution fusion | flops 562036736 | bytes 4521984 | tf_op jit(solution)/shard_map/hts,shp->thp/dot_general | solution.py:667
  169.0 3.1 %copy.59 = f32[512,1024]{1,0:T(8,128)} copy(f32[512,1024]{0,1:T(8,128)} %bitcast.43) | data formatting | bytes 4194304 | tf_op jit(solution)/shard_map/reshape | solution.py:667
  172.2 1.6 broadcast_in_dim.167
  173.8 2.9 %copy.58 = f32[512,1024]{1,0:T(8,128)} copy(f32[512,1024]{0,1:T(8,128)} %bitcast.42) | data formatting | bytes 4194304 | tf_op jit(solution)/shard_map/reshape | solution.py:677
  177.0 20.7 %all-gather.2.cloned.1.call-done = bf16[4,16,16512]{2,1,0:T(8,128)(2,1)} async-done(((bf16[1,16,16512]{2,1,0:T(8,128)(2,1)}), bf16[4,16,16512]{2,1,0:T(8,128)(2,1)}) %all-gather.2.cloned.1.call-update) | async-done | bytes 2113552 | tf_op jit(solution)/shard_map/all_gather | solution.py:659
  197.6 1.9 convert_element_type.99
  200.1 0.4 fusion.10
  200.8 3.8 %multiply_reduce_fusion = (f32[512]{0:T(512)S(1)}, f32[512,1024]{1,0:T(8,128)S(1)}) fusion(bf16[528,1280]{1,0:T(8,128)(2,1)} %get-tuple-element.11, bf16[512,1024]{1,0:T(8,128)(2,1)S(1)} %multiply_convert_fusion.3, f32[1024]{0:T(1024)S(1)} %mul.307, f32[512,1024]{1,0:T(8,128)} %copy.59, f32[512,1024]{1,0:T(8,128)} %copy.58, ...), kind=kOutput, calls=%fused_computation.14 | convolution fusion | flops 275250688 | bytes 9181184 | tf_op jit(solution)/shard_map/dot_general | solution.py:677
  204.6 0.2 multiply_convert_fusion.2.normed_ref
  204.8 44.2 %shard_map.119 = bf16[64,4096]{1,0:T(8,128)(2,1)S(1)} custom-call(bf16[512,1024]{1,0:T(8,128)(2,1)S(1)} %multiply_convert_fusion.2.normed_ref, bf16[4096,2048]{1,0:T(8,128)(2,1)} %w_hbm.3), custom_call_target="tpu_custom_call" | custom-call | tf_op jit(solution)/shard_map/pallas_call | solution.py:582
  249.0 0.8 copy.61
  (41 shorter events, 2.8 us)
Async XLA Ops:
  6.5 191.1 %all-gather.2.cloned.1.call-start = ((), (), s32[]{:S(2)}) async-start(), calls=%async_computation | async-start | bytes 2641920 | tf_op jit(solution)/shard_map/all_gather | solution.py:659
  153.4 1.9 copy-start.6
  153.4 2.0 copy-start.5
  153.4 2.1 copy-start
  155.5 2.1 copy-start.4
  157.6 1.6 copy-start.1
  160.1 1.6 copy-start.3
  169.0 3.1 %copy-start.2 = (f32[512,16]{1,0:T(8,128)S(1)}, f32[512,16]{1,0:T(8,128)}, u32[]{:S(2)}) copy-start(f32[512,16]{1,0:T(8,128)} %get-tuple-element.18) | copy-start | bytes 98308
  173.8 2.9 %copy-start.7 = (f32[32]{0:T(128)S(1)}, f32[32]{0:T(128)}, u32[]{:S(2)}) copy-start(f32[32]{0:T(128)} %param.22) | copy-start | bytes 388
  200.7 3.8 %dynamic-slice-start = ((f32[2048]{0:T(1024)}, s32[]{:T(128)}), f32[1024]{0:T(1024)S(1)}, s32[]{:S(2)}) async-start(f32[2048]{0:T(1024)} %param.23, s32[]{:T(128)} %select_n.111), calls=%async_computation.1 | async-start | bytes 8704 | tf_op jit(solution)/shard_map/dynamic_slice | solution.py:616
Sparse Core Ops, SparseCore 0:
  161.2 36.4 all-gather.1

commit v3 on v2

--- a/solution.py
+++ b/solution.py
@@ -598,90 +598,237 @@
     )(normed, w_out)
 
 
+def scan_kernel(
+    xb_ref, dt_ref, zc_ref, metas, tapx_ref, tapbc_ref, head_ref, chan_ref,
+    normed_ref,
+    xs, bs, cs, bt, cum_t, dt_t, w_t, bias, scores, ssd, gz, entry, square, state, got, inc,
+    send_sem, recv_sem,
+):
+    f32, bf = jnp.float32, jnp.bfloat16
+    me = lax.axis_index("dp")
+    core, chip = me % 2, me // 2
+    block, chans = normed_ref.shape
+    rows = block // 2
+    wide = bs.shape[1]
+
+    barrier = pltpu.get_barrier_semaphore()
+    for k in range(1, 4):
+        pl.semaphore_signal(
+            barrier, inc=1, device_id={"dp": (me + 2 * k) % 8}, device_id_type=MESH
+        )
+    pl.semaphore_wait(barrier, 3)
+
+    first, second = metas[2 * chip, 1:2, :], metas[2 * chip + 1, 1:2, :]
+    earlier = metas[(2 * chip + 7) % 8, 1:2, :]
+    follows = (chip + 3) // 4
+    earlier = earlier * follows - (1 - follows)
+
+    def column(row):
+        return jnp.broadcast_to(row, (128, row.shape[1])).T
+
+    seg_ext = jnp.concatenate(
+        [column(earlier)[rows - HALO :], column(first), column(second)], axis=0
+    )
+    seg_row = jnp.concatenate([first, second], axis=1)
+    seg_col = seg_ext[HALO:]
+    seg_before = seg_ext[HALO - 1 : HALO]
+    seg_last = seg_ext[block + HALO - 1 :]
+    same = [jnp.where(pltpu.roll(seg_ext, k, 0) == seg_ext, 1.0, 0.0) for k in range(1, CONV)]
+
+    def convolved(src, col, taps):
+        v = src[:, pl.ds(col, 128)].astype(f32)
+        total = taps[CONV - 1 : CONV] * v
+        for k in range(1, CONV):
+            total = total + same[k - 1] * (taps[CONV - 1 - k : CONV - k] * pltpu.roll(v, k, 0))
+        total = total[HALO:]
+        return (total / (1.0 + jnp.exp(-total))).astype(bf)
+
+    @pl.loop(0, chans // 128)
+    def _(t):
+        col = pl.multiple_of(t * 128, 128)
+        xs[:, pl.ds(col, 128)] = convolved(
+            xb_ref, col, tapx_ref[:, pl.ds(pl.multiple_of(core * chans + col, 128), 128)]
+        )
+
+    for t in range(wide // 128):
+        at = pl.ds(pl.multiple_of(core * wide + t * 128, 128), 128)
+        here = pl.ds(t * 128, 128)
+        bs[:, here] = convolved(xb_ref, chans + t * 128, tapbc_ref[0, :, at])
+        cs[:, here] = convolved(zc_ref, chans + t * 128, tapbc_ref[1, :, at])
+    bt[...] = bs[...].astype(f32).T.astype(bf)
+
+    heads = head_ref[core]
+    u = dt_ref[HALO:, :] + heads[0:1]
+    step_dt = jnp.maximum(u, 0.0) + jnp.log1p(jnp.exp(-jnp.abs(u)))
+    rate = -step_dt * heads[1:2]
+    lower = jnp.where(
+        lax.broadcasted_iota(jnp.int32, (block, block), 0)
+        >= lax.broadcasted_iota(jnp.int32, (block, block), 1), 1.0, 0.0
+    ).astype(bf)
+    high = rate.astype(bf)
+    middle = (rate - high.astype(f32)).astype(bf)
+    low = (rate - high.astype(f32) - middle.astype(f32)).astype(bf)
+    cum = (
+        jnp.dot(lower, high, preferred_element_type=f32)
+        + jnp.dot(lower, middle, preferred_element_type=f32)
+        + jnp.dot(lower, low, preferred_element_type=f32)
+    )
+    cum_t[...] = cum.T
+    dt_t[...] = step_dt.T
+    at_last = jnp.where(seg_row == seg_row[:, block - 1 :], 1.0, 0.0)
+    w_t[...] = jnp.exp(cum_t[:, block - 1 :] - cum_t[...]) * dt_t[...] * at_last
+    enters = jnp.where(seg_col == seg_before, 1.0, 0.0)
+    keeps = jnp.where(seg_last == seg_before, 1.0, 0.0)
+
+    def pair_rows(ref, p):
+        return ref[pl.ds(2 * p, 1), :], ref[pl.ds(2 * p + 1, 1), :]
+
+    def pair_column(ref, p):
+        a, b = pair_rows(ref, p)
+        return jnp.concatenate(
+            [jnp.broadcast_to(a, (64, block)), jnp.broadcast_to(b, (64, block))], axis=0
+        ).T
+
+    @pl.loop(0, chans // 128)
+    def _(p):
+        cols = pl.ds(pl.multiple_of(p * 128, 128), 128)
+        weighted = (pair_column(w_t, p) * xs[:, cols].astype(f32)).astype(bf)
+        state[0:wide, cols] = jnp.dot(
+            bt[...], weighted, preferred_element_type=f32
+        ).astype(bf)
+        reach = jnp.exp(pair_column(cum_t, p))
+        gain = jnp.broadcast_to(reach[block - 1 :] * keeps, (8, 128))
+        rounded = gain.astype(bf).astype(f32)
+        state[wide : wide + 16, cols] = jnp.concatenate([rounded, gain - rounded], axis=0).astype(bf)
+        entry[:, cols] = reach * enters
+
+    def leave(to):
+        return remote(
+            state, got.at[chip % 3], send_sem.at[to - 1], recv_sem.at[chip % 3], 2 * to + core
+        )
+
+    for to in (3, 2, 1):
+
+        @pl.when(chip < to)
+        def _():
+            leave(to).start()
+
+    scores[...] = jnp.dot(cs[...], bt[...], preferred_element_type=f32)
+    for t in range(block // 128):
+        here = slice(t * 128, (t + 1) * 128)
+        linked = (seg_col == seg_row[:, here]) & (
+            lax.broadcasted_iota(jnp.int32, (block, 128), 0)
+            >= lax.broadcasted_iota(jnp.int32, (block, 128), 1) + t * 128
+        )
+        bias[:, here] = jnp.where(linked, 0.0, -1e30)
+
+    lanes = lax.broadcasted_iota(jnp.int32, (rows, 128), 1)
+
+    @pl.loop(0, chans // 128)
+    def _(p):
+        cols = pl.ds(pl.multiple_of(p * 128, 128), 128)
+        at = pl.ds(pl.multiple_of(core * chans + p * 128, 128), 128)
+        cum_rows, dt_rows = pair_rows(cum_t, p), pair_rows(dt_t, p)
+        cum_cols = [column(r) for r in cum_rows]
+        for i in range(2):
+            here = slice(i * rows, (i + 1) * rows)
+            w = (i + 1) * rows
+            outs = []
+            for n in range(2):
+                spans = jnp.concatenate([cum_cols[n][here]] * (w // 128), axis=1)
+                spans = spans - cum_rows[n][:, :w] + bias[here, :w]
+                mixing = (scores[here, :w] * jnp.exp(spans) * dt_rows[n][:, :w]).astype(bf)
+                outs.append(jnp.dot(mixing, xs[0:w, cols], preferred_element_type=f32))
+            ssd[here, cols] = jnp.where(lanes < 64, outs[0], outs[1]) + chan_ref[
+                0:1, at
+            ] * xs[here, cols].astype(f32)
+        z = zc_ref[:, cols].astype(f32)[HALO:]
+        gz[:, cols] = z / (1.0 + jnp.exp(-z))
+
+    inc[...] = jnp.zeros_like(inc)
+    for source in range(3):
+
+        @pl.when(source < chip)
+        def _():
+            remote(
+                state, got.at[source], send_sem.at[0], recv_sem.at[source], (me + 2) % 8
+            ).wait_recv()
+            gain = (
+                got[source, wide : wide + 8, :].astype(f32)
+                + got[source, wide + 8 : wide + 16, :].astype(f32)
+            )[0:1]
+            inc[...] = gain * inc[...] + got[source, 0:wide, :].astype(f32)
+
+    square[...] = jnp.zeros_like(square)
+
+    @pl.loop(0, chans // 128)
+    def _(p):
+        cols = pl.ds(pl.multiple_of(p * 128, 128), 128)
+        before = jnp.dot(cs[...], inc[:, cols].astype(bf), preferred_element_type=f32)
+        gated = (ssd[:, cols] + entry[:, cols] * before) * gz[:, cols]
+        ssd[:, cols] = gated
+        square[...] += gated * gated
+
+    inv = lax.rsqrt(jnp.sum(square[...], axis=1, keepdims=True) * (1.0 / chans) + 1e-05)
+    inv = jnp.broadcast_to(inv, (block, 128))
+
+    @pl.loop(0, chans // 128)
+    def _(p):
+        cols = pl.ds(pl.multiple_of(p * 128, 128), 128)
+        at = pl.ds(pl.multiple_of(core * chans + p * 128, 128), 128)
+        normed_ref[:, cols] = (ssd[:, cols] * inv * chan_ref[1:2, at]).astype(bf)
+
+    for to in (3, 2, 1):
+
+        @pl.when(chip < to)
+        def _():
+            leave(to).wait_send()
+
+
+def scan(xb, dt_raw, zc, metas, conv_x, conv_bc, heads, chan):
+    f32, bf = jnp.float32, jnp.bfloat16
+    block = xb.shape[0] - HALO
+    chans = conv_x.shape[1] // 2
+    wide = xb.shape[1] - chans
+    dma = pltpu.SemaphoreType.DMA
+    vmem = pl.BlockSpec(memory_space=pltpu.VMEM)
+
+    def buf(shape, kind=f32):
+        return pltpu.VMEM(shape, kind)
+
+    return pl.pallas_call(
+        scan_kernel,
+        out_shape=jax.ShapeDtypeStruct((block, chans), bf),
+        in_specs=[vmem] * 8,
+        out_specs=vmem,
+        scratch_shapes=[
+            buf((block, chans), bf), buf((block, wide), bf), buf((block, wide), bf),
+            buf((wide, block), bf),
+            buf((128, block)), buf((128, block)), buf((128, block)),
+            buf((block, block)), buf((block, block)),
+            buf((block, chans)), buf((block, chans)), buf((block, chans)), buf((block, 128)),
+            buf((wide + 16, chans), bf), buf((3, wide + 16, chans), bf), buf((wide, chans)),
+            dma((3,)), dma((3,)),
+        ],
+        compiler_params=pltpu.CompilerParams(
+            collective_id=2, has_side_effects=True, vmem_limit_bytes=40 << 20
+        ),
+    )(xb, dt_raw, zc, metas, conv_x, conv_bc, heads, chan)
+
+
 def on_plane(
     tokens, pack_source, segment_ids, w_in, w_dt, w_out, conv_x, conv_bc,
     dt_bias, decay_rate, skip_gain, norm_gain,
 ):
-    f32, bf = jnp.float32, jnp.bfloat16
-    rows = tokens.shape[0]
-    total = 8 * rows
-    block = 2 * rows
-    me = lax.axis_index("dp")
-    core, chip = me % 2, me // 2
     heads = w_dt.shape[1] // 2
-    chans = w_out.shape[1] // 2
-
-    def mine(values, axis):
-        size = values.shape[axis] // 2
-        return lax.dynamic_slice_in_dim(values, core * size, size, axis)
-
     meta = jnp.pad(jnp.stack([pack_source, segment_ids]), ((0, 6), (0, 0)))
     halves = w_dt.reshape(w_dt.shape[0], 2, heads).transpose(1, 0, 2)
     wdt = jnp.pad(jnp.concatenate([halves, halves], axis=2), ((0, 0), (0, 0), (0, 128 - 2 * heads)))
     xb, dt_raw, zc, metas = project(tokens, meta, w_in, wdt)
-    seg_all = jnp.concatenate([jnp.full((HALO,), -1, jnp.int32), metas[:, 1, :].reshape(total)])
-    seg_ext = lax.dynamic_slice_in_dim(seg_all, chip * block, block + HALO, 0)
-    seg = seg_ext[HALO:]
-    seg_before = seg_ext[HALO - 1]
-    taps_bc = mine(conv_bc, 2)
-
-    def convolve(values, taps):
-        total_sum = jnp.zeros((block, values.shape[1]), f32)
-        for lag in range(CONV):
-            first = HALO - CONV + 1 + lag
-            same = (seg_ext[first : first + block] == seg)[:, None]
-            total_sum = total_sum + jnp.where(
-                same, taps[lag][None, :] * values[first : first + block].astype(f32), 0.0
-            )
-        return jax.nn.silu(total_sum).astype(bf)
-
-    x = convolve(xb[:, :chans], mine(conv_x, 1))
-    b = convolve(xb[:, chans:], taps_bc[:, 0])
-    c = convolve(zc[:, chans:], taps_bc[:, 1])
-    gate = jax.nn.silu(zc[HALO:, :chans].astype(f32))
-    step_dt = jax.nn.softplus(dt_raw[HALO:, :heads] + mine(dt_bias, 0))
-    step_rate = -step_dt * mine(decay_rate, 0)
-    places = jnp.arange(block)
-    lower = (places[:, None] >= places[None, :])
-    cum = jnp.dot(lower.astype(f32), step_rate, precision=highest)
-    xh = x.reshape(block, heads, HEAD_DIM)
-
-    last = seg[-1]
-    weight = jnp.where((seg == last)[:, None], jnp.exp(cum[-1][None, :] - cum), 0.0) * step_dt
-    wide = jnp.repeat(weight, HEAD_DIM, axis=1)
-    weighted = (wide * x.astype(f32)).astype(bf)
-    left = lax.dot_general(weighted, b, (((0,), (0,)), ((), ())), preferred_element_type=f32)
-    gain = jnp.where(last == seg_before, jnp.exp(cum[-1]), 0.0)
-    sent = jnp.concatenate(
-        [left.reshape(heads, HEAD_DIM * STATE), jnp.broadcast_to(gain[:, None], (heads, 128))], axis=1
-    ).astype(bf)
-    groups = [[i, i + 2, i + 4, i + 6] for i in range(2)]
-    gathered = lax.all_gather(sent, "dp", axis_index_groups=groups).astype(f32)
-
-    linked = (seg[:, None] == seg[None, :]) & lower
-    cum_t = cum.T
-    spans = cum_t[:, :, None] - cum_t[:, None, :]
-    decay = jnp.where(linked[None], jnp.exp(jnp.where(linked[None], spans, 0.0)), 0.0)
-    scores = lax.dot_general(c, b, (((1,), (1,)), ((), ())), preferred_element_type=f32)
-    mixing = (scores[None] * decay * step_dt.T[:, None, :]).astype(bf)
-    ssd = jnp.einsum("hts,shp->thp", mixing, xh, preferred_element_type=f32).reshape(block, chans)
-
-    incoming = jnp.zeros((heads, HEAD_DIM * STATE), f32)
-    for k in range(3):
-        part = gathered[k]
-        incoming = jnp.where(
-            k < chip, part[:, -1:] * incoming + part[:, : HEAD_DIM * STATE], incoming
-        )
-    before = incoming.reshape(chans, STATE).astype(bf)
-    entry = jnp.where((seg == seg_before)[:, None], jnp.exp(cum), 0.0)
-    ssd = ssd + jnp.repeat(entry, HEAD_DIM, axis=1) * lax.dot_general(
-        c, before, (((1,), (1,)), ((), ())), preferred_element_type=f32
-    )
-    skip = jnp.repeat(mine(skip_gain, 0), HEAD_DIM)[None, :]
-    gated = (ssd + skip * x.astype(f32)) * gate
-    inv = lax.rsqrt(jnp.mean(gated * gated, axis=1, keepdims=True) + 1e-05)
-    normed = (gated * inv * mine(norm_gain, 0)[None, :]).astype(bf)
-
+    params = jnp.stack([dt_bias, decay_rate]).reshape(2, 2, heads).transpose(1, 0, 2)
+    params = jnp.pad(params, ((0, 0), (0, 6), (0, 128 - heads)))
+    chan = jnp.stack([jnp.repeat(skip_gain, HEAD_DIM), norm_gain])
+    normed = scan(xb, dt_raw, zc, metas, conv_x, conv_bc.transpose(1, 0, 2), params, chan)
     return project_out(normed, w_out)
 
 

time: 257 us -> 228 us (0.89)
  Pallas kernels: 178 us -> 216 us
  waiting for transfers between devices: 20.7 us -> 0 us
  between operations: 15 us -> 0.06 us
  matrix products: 13.1 us -> 0 us
  other arithmetic: 12 us -> 2.27 us
  local copies, waits for them, and re-layouts: 18.1 us -> 9.77 us
    pallas_call x0 -> x1, Pallas kernels: none -> 37.7 us  [scan(): pl.pallas_call(scan_kernel, out_shape=jax.ShapeDtypeStruct((block, chans)...]
    all_gather x1 -> x0, waiting for transfers between devices: 20.7 us -> none  [on_plane(): gathered = lax.all_gather(sent, 'dp', axis_index_groups=groups).astype(f32)]
    dot_general x5 -> x0, matrix products: 13.1 us -> none  [the longest x1 6.71 us: on_plane(): jnp.einsum('hts,shp->thp', mixing, xh, preferred_element_type=f32)]
    reshape x3 -> x0, local copies, waits for them, and re-layouts: 7.87 us -> none  [the longest x1 3.08 us: on_plane(): jnp.einsum('hts,shp->thp', mixing, xh, preferred_element_type=f32)]
    convert_element_type x5 -> x0, other arithmetic: 5.79 us -> none  [the longest x2 3.28 us: convolve(): return jax.nn.silu(total_sum).astype(bf)]
    unnamed x17 -> x12, local copies, waits for them, and re-layouts: 1.2 us -> 5.97 us
  transfers between devices with their start and end apart: 1 -> 0, of which waited for: 1 -> 0; matrix products, arithmetic and copies ran while one was open for 6% -> 0% of each run, Pallas kernels for 0% -> 0%
where the time goes in v3:
time: 228 us
  Pallas kernels  216 us (95%)
  local copies, waits for them, and re-layouts  9.77 us (4%)
    pallas_call x1, Pallas kernels, project(): pl.pallas_call(projection_kernel, out_shape=(jax.ShapeDtypeStruct((m, na)...  134 us
    pallas_call x1, Pallas kernels, project_out(): pl.pallas_call(output_kernel, out_shape=jax.ShapeDtypeStruct((half // 4,...  44.3 us
    pallas_call x1, Pallas kernels, scan(): pl.pallas_call(scan_kernel, out_shape=jax.ShapeDtypeStruct((block, chans)...  37.7 us
    unnamed x12, local copies, waits for them, and re-layouts  5.97 us

profile of v3, /device:TPU:20, one launch (start us, length us, event | category | flops | bytes accessed | tf_op | source)
XLA Modules:
  0.0 227.6 jit_solution(14884549493049449398)
XLA Ops:
  0.0 0.7 stack.27
  0.7 0.7 stack.28
  1.5 0.7 pad_add_fusion
  2.2 0.6 pad.12.meta_ref
  2.8 0.7 copy.25
  3.5 0.7 broadcast_in_dim.3
  4.2 0.1 stack_reshape.3
  4.3 0.7 pad_maximum_fusion.1.chan_ref
  5.0 0.8 pad_maximum_fusion
  5.9 0.2 copy.20
  6.1 0.8 pad.13.wdt_ref
  6.8 0.0 copy-start.4
  6.8 133.6 %shard_map.118 = (bf16[528,1280]{1,0:T(8,128)(2,1)}, f32[528,128]{1,0:T(8,128)}, bf16[528,1280]{1,0:T(8,128)(2,1)}, s32[8,8,256]{2,1,0:T(8,128)}) custom-call(bf16[256,4096]{1,0:T(8,128)(2,1)} %tok_hbm.1, s32[8,256]{1,0:T(8,128)} %pad.12.meta_ref, bf16[512,5120]{1,0:T(8,128)(2,1)} %w_hbm.2, bf16[2,512,128]{2,1,0:T(8,128)(2,1)} %pad.13.wdt_ref), custom_call_target="tpu_custom_call" | custom-call | tf_op jit(solution)/shard_map/pallas_call | solution.py:437
  140.4 0.0 copy-done.4
  140.4 0.0 copy-start
  140.5 1.3 copy-done
  141.8 0.0 copy-start.1
  141.8 1.3 copy-done.1
  143.1 0.0 copy-start.2
  143.1 1.0 copy-done.2
  144.1 0.0 copy-start.3
  144.1 0.8 copy-done.3
  144.9 37.7 %shard_map.119.normed_ref = bf16[512,1024]{1,0:T(8,128)(2,1)S(1)} custom-call(bf16[528,1280]{1,0:T(8,128)(2,1)S(1)} %copy-done, f32[528,128]{1,0:T(8,128)S(1)} %copy-done.2, bf16[528,1280]{1,0:T(8,128)(2,1)S(1)} %copy-done.1, s32[8,8,256]{2,1,0:T(8,128)S(1)} %copy-done.3, f32[4,2048]{1,0:T(4,128)S(1)} %copy-done.4, f32[2,4,512]{2,1,0:T(4,128)S(1)} %bitcast.13, ...), custom_call_target="tpu_custom_call" | custom-call | tf_op jit(solution)/shard_map/pallas_call | solution.py:799
  182.6 44.3 %shard_map.120 = bf16[64,4096]{1,0:T(8,128)(2,1)S(1)} custom-call(bf16[512,1024]{1,0:T(8,128)(2,1)S(1)} %shard_map.119.normed_ref, bf16[4096,2048]{1,0:T(8,128)(2,1)} %w_hbm.3), custom_call_target="tpu_custom_call" | custom-call | tf_op jit(solution)/shard_map/pallas_call | solution.py:582
  226.8 0.8 copy.27
  (2 shorter events, 0.0 us)
Async XLA Ops:
  6.8 133.6 %copy-start.4 = (f32[4,2048]{1,0:T(4,128)S(1)}, f32[4,2048]{1,0:T(4,128)}, u32[]{:S(2)}) copy-start(f32[4,2048]{1,0:T(4,128)} %tapx_ref.1) | copy-start | bytes 98308
  140.4 1.3 copy-start
  141.8 1.3 copy-start.1
  143.1 1.0 copy-start.2
  144.1 0.8 copy-start.3

commit v4 on v3

--- a/solution.py
+++ b/solution.py
@@ -206,13 +206,13 @@
 
 
 def projection_kernel(
-    tok_hbm, meta_ref, w_hbm, wdt_ref,
+    tok_hbm, source_ref, segment_ref, w_hbm, wdt_ref,
     xb_out, dt_out, zc_out, meta_out,
-    tokg, metas, wbuf, idxcol, onehot, packed, own,
+    meta_ref, tokg, metas, wbuf, idxcol, onehot, packed, own,
     s_da, s_db, s_xa, s_yb, s_ya, s_xb,
     r_da, r_db, r_xa, r_yb, r_sa, r_sb,
     loc_sem, meta_send, meta_recv, w_send, w_recv,
-    tok_send, tok_recv, fwd_send, fwd_recv, red_send, red_recv,
+    tok_send, tok_recv, z_send, z_recv, fwd_send, fwd_recv, red_send, red_recv,
 ):
     me = lax.axis_index("dp")
     core = me % 2
@@ -234,7 +234,13 @@
     barrier = pltpu.get_barrier_semaphore()
     for k in range(1, 8):
         pl.semaphore_signal(barrier, inc=1, device_id={"dp": (me + k) % 8}, device_id_type=MESH)
-    pl.semaphore_wait(barrier, 7)
+    m = lax.axis_index("mp")
+    beside = m + 1 - 2 * (m % 2)
+    pl.semaphore_signal(barrier, inc=1, device_id={"mp": beside}, device_id_type=MESH)
+    meta_ref[...] = jnp.concatenate(
+        [source_ref[...], segment_ref[...], jnp.zeros((6, rows), jnp.int32)], axis=0
+    )
+    pl.semaphore_wait(barrier, 8)
 
     mine = pl.ds(pl.multiple_of(me * rows, rows), rows)
 
@@ -246,11 +252,19 @@
         copies.append(
             remote(meta_ref, metas.at[me], meta_send.at[k - 1], meta_recv.at[k - 1], (me + k) % 8)
         )
+    part = rows // 2
+    half = m % 2
+
+    def halves(dev, which):
+        return pl.ds(pl.multiple_of(dev * rows + which * part, part), part)
+
     directs = []
     for i, to in enumerate((chip_d, chip_x, chip_y)):
         directs.append(
-            remote(tok_hbm.at[:, columns(to)], tokg.at[mine], tok_send.at[i], tok_recv.at[i],
-                   2 * to + core)
+            remote(
+                tok_hbm.at[pl.ds(pl.multiple_of(half * part, part), part), columns(to)],
+                tokg.at[halves(me, half)], tok_send.at[i], tok_recv.at[i], 2 * to + core,
+            )
         )
     for c in copies + directs:
         c.start()
@@ -294,10 +308,25 @@
         idxcol[HALO + j * rows : HALO + (j + 1) * rows, :] = jnp.broadcast_to(row, (128, rows)).T
     meta_out[...] = metas[...]
 
-    for i, source in enumerate((chip_d, chip_x, chip_y)):
+    sources = [2 * to + core for to in (chip_d, chip_x, chip_y)]
+    across = []
+    for i, dev in enumerate(sources):
         directs[i].wait_recv()
-        theirs = pl.ds(pl.multiple_of((2 * source + core) * rows, rows), rows)
-        c = remote(tokg.at[theirs], tokg.at[theirs], fwd_send.at[1 + i], fwd_recv.at[1 + i], sibling)
+        there = tokg.at[halves(dev, half)]
+        across.append(
+            pltpu.make_async_remote_copy(
+                src_ref=there, dst_ref=there, send_sem=z_send.at[i], recv_sem=z_recv.at[i],
+                device_id={"mp": beside}, device_id_type=MESH,
+            )
+        )
+        across[i].start()
+        c = remote(there, there, fwd_send.at[1 + i], fwd_recv.at[1 + i], sibling)
+        c.start()
+        forward.append(c)
+    for i, dev in enumerate(sources):
+        across[i].wait_recv()
+        there = tokg.at[halves(dev, 1 - half)]
+        c = remote(there, there, fwd_send.at[4 + i], fwd_recv.at[4 + i], sibling)
         c.start()
         forward.append(c)
     for c in local[:1] + local[2:]:
@@ -419,11 +448,11 @@
             own[:, own_cols] + r_yb[:, cols].astype(jnp.float32) + r_sb[:, cols].astype(jnp.float32)
         ).astype(jnp.bfloat16)
 
-    for c in copies + directs + forward + weights + [c_da, c_db, c_xa, c_yb, c_ya, c_xb]:
+    for c in copies + directs + across + forward + weights + [c_da, c_db, c_xa, c_yb, c_ya, c_xb]:
         c.wait_send()
 
 
-def project(tokens, meta, w_in, wdt):
+def project(tokens, source, segment, w_in, wdt):
     rows, depth = tokens.shape[0], w_in.shape[0]
     width = w_in.shape[1] // 5
     na = width + width // 4
@@ -442,9 +471,10 @@
             jax.ShapeDtypeStruct((m, nb), bf),
             jax.ShapeDtypeStruct((8, 8, rows), jnp.int32),
         ),
-        in_specs=[hbm, vmem, hbm, vmem],
+        in_specs=[hbm, vmem, vmem, hbm, vmem],
         out_specs=(vmem,) * 4,
         scratch_shapes=[
+            pltpu.VMEM((8, rows), jnp.int32),
             pltpu.VMEM((8 * rows, 2 * depth), bf),
             pltpu.VMEM((8, 8, rows), jnp.int32),
             pltpu.VMEM((2 * depth, na + 128 + nb), bf),
@@ -455,12 +485,12 @@
             a, b, a, b, a, b,
             a, b, a, b, a, b,
             dma((7,)), dma((7,)), dma((7,)), dma((5,)), dma((5,)),
-            dma((3,)), dma((3,)), dma((4,)), dma((4,)), dma((6,)), dma((6,)),
+            dma((3,)), dma((3,)), dma((3,)), dma((3,)), dma((7,)), dma((7,)), dma((6,)), dma((6,)),
         ],
         compiler_params=pltpu.CompilerParams(
             collective_id=0, has_side_effects=True, vmem_limit_bytes=58 << 20
         ),
-    )(tokens, meta, w_in, wdt)
+    )(tokens, source, segment, w_in, wdt)
 
 
 TILES = 4
@@ -599,7 +629,7 @@
 
 
 def scan_kernel(
-    xb_ref, dt_ref, zc_ref, metas, tapx_ref, tapbc_ref, head_ref, chan_ref,
+    xb_ref, dt_ref, zc_ref, metas, tapx_ref, tapbc_ref, head_ref, skip_ref, chan_ref,
     normed_ref,
     xs, bs, cs, bt, cum_t, dt_t, w_t, bias, scores, ssd, gz, entry, square, state, got, inc,
     send_sem, recv_sem,
@@ -608,6 +638,7 @@
     me = lax.axis_index("dp")
     core, chip = me % 2, me // 2
     block, chans = normed_ref.shape
+    heads_here = chans // HEAD_DIM
     rows = block // 2
     wide = bs.shape[1]
 
@@ -653,8 +684,8 @@
     for t in range(wide // 128):
         at = pl.ds(pl.multiple_of(core * wide + t * 128, 128), 128)
         here = pl.ds(t * 128, 128)
-        bs[:, here] = convolved(xb_ref, chans + t * 128, tapbc_ref[0, :, at])
-        cs[:, here] = convolved(zc_ref, chans + t * 128, tapbc_ref[1, :, at])
+        bs[:, here] = convolved(xb_ref, chans + t * 128, tapbc_ref[:, 0, at])
+        cs[:, here] = convolved(zc_ref, chans + t * 128, tapbc_ref[:, 1, at])
     bt[...] = bs[...].astype(f32).T.astype(bf)
 
     heads = head_ref[core]
@@ -727,7 +758,6 @@
     @pl.loop(0, chans // 128)
     def _(p):
         cols = pl.ds(pl.multiple_of(p * 128, 128), 128)
-        at = pl.ds(pl.multiple_of(core * chans + p * 128, 128), 128)
         cum_rows, dt_rows = pair_rows(cum_t, p), pair_rows(dt_t, p)
         cum_cols = [column(r) for r in cum_rows]
         for i in range(2):
@@ -739,9 +769,12 @@
                 spans = spans - cum_rows[n][:, :w] + bias[here, :w]
                 mixing = (scores[here, :w] * jnp.exp(spans) * dt_rows[n][:, :w]).astype(bf)
                 outs.append(jnp.dot(mixing, xs[0:w, cols], preferred_element_type=f32))
-            ssd[here, cols] = jnp.where(lanes < 64, outs[0], outs[1]) + chan_ref[
-                0:1, at
-            ] * xs[here, cols].astype(f32)
+            skips = jnp.where(
+                lanes < 64, skip_ref[core * heads_here + 2 * p], skip_ref[core * heads_here + 2 * p + 1]
+            )
+            ssd[here, cols] = (
+                jnp.where(lanes < 64, outs[0], outs[1]) + skips * xs[here, cols].astype(f32)
+            )
         z = zc_ref[:, cols].astype(f32)[HALO:]
         gz[:, cols] = z / (1.0 + jnp.exp(-z))
 
@@ -776,7 +809,7 @@
     def _(p):
         cols = pl.ds(pl.multiple_of(p * 128, 128), 128)
         at = pl.ds(pl.multiple_of(core * chans + p * 128, 128), 128)
-        normed_ref[:, cols] = (ssd[:, cols] * inv * chan_ref[1:2, at]).astype(bf)
+        normed_ref[:, cols] = (ssd[:, cols] * inv * chan_ref[0:1, at]).astype(bf)
 
     for to in (3, 2, 1):
 
@@ -785,7 +818,7 @@
             leave(to).wait_send()
 
 
-def scan(xb, dt_raw, zc, metas, conv_x, conv_bc, heads, chan):
+def scan(xb, dt_raw, zc, metas, conv_x, conv_bc, heads, skip, chan):
     f32, bf = jnp.float32, jnp.bfloat16
     block = xb.shape[0] - HALO
     chans = conv_x.shape[1] // 2
@@ -799,7 +832,7 @@
     return pl.pallas_call(
         scan_kernel,
         out_shape=jax.ShapeDtypeStruct((block, chans), bf),
-        in_specs=[vmem] * 8,
+        in_specs=[vmem] * 7 + [pl.BlockSpec(memory_space=pltpu.SMEM), vmem],
         out_specs=vmem,
         scratch_shapes=[
             buf((block, chans), bf), buf((block, wide), bf), buf((block, wide), bf),
@@ -813,7 +846,7 @@
         compiler_params=pltpu.CompilerParams(
             collective_id=2, has_side_effects=True, vmem_limit_bytes=40 << 20
         ),
-    )(xb, dt_raw, zc, metas, conv_x, conv_bc, heads, chan)
+    )(xb, dt_raw, zc, metas, conv_x, conv_bc, heads, skip, chan)
 
 
 def on_plane(
@@ -821,14 +854,16 @@
     dt_bias, decay_rate, skip_gain, norm_gain,
 ):
     heads = w_dt.shape[1] // 2
-    meta = jnp.pad(jnp.stack([pack_source, segment_ids]), ((0, 6), (0, 0)))
     halves = w_dt.reshape(w_dt.shape[0], 2, heads).transpose(1, 0, 2)
     wdt = jnp.pad(jnp.concatenate([halves, halves], axis=2), ((0, 0), (0, 0), (0, 128 - 2 * heads)))
-    xb, dt_raw, zc, metas = project(tokens, meta, w_in, wdt)
+    xb, dt_raw, zc, metas = project(
+        tokens, pack_source.reshape(1, -1), segment_ids.reshape(1, -1), w_in, wdt
+    )
     params = jnp.stack([dt_bias, decay_rate]).reshape(2, 2, heads).transpose(1, 0, 2)
     params = jnp.pad(params, ((0, 0), (0, 6), (0, 128 - heads)))
-    chan = jnp.stack([jnp.repeat(skip_gain, HEAD_DIM), norm_gain])
-    normed = scan(xb, dt_raw, zc, metas, conv_x, conv_bc.transpose(1, 0, 2), params, chan)
+    normed = scan(
+        xb, dt_raw, zc, metas, conv_x, conv_bc, params, skip_gain, norm_gain.reshape(1, -1)
+    )
     return project_out(normed, w_out)
 
 

time: 228 us -> 226 us (level)
    unnamed x12 -> x17, local copies, waits for them, and re-layouts: 5.97 us -> 5.26 us
where the time goes in v4:
time: 226 us; the launch traced here: 225 us
  Pallas kernels  216 us (96%)
  local copies, waits for them, and re-layouts  7.66 us (3%)
    pallas_call x1, Pallas kernels, project(): pl.pallas_call(projection_kernel, out_shape=(jax.ShapeDtypeStruct((m, na)...  135 us
    pallas_call x1, Pallas kernels, project_out(): pl.pallas_call(output_kernel, out_shape=jax.ShapeDtypeStruct((half // 4,...  43.4 us
    pallas_call x1, Pallas kernels, scan(): pl.pallas_call(scan_kernel, out_shape=jax.ShapeDtypeStruct((block, chans)...  37.8 us
    unnamed x17, local copies, waits for them, and re-layouts  5.26 us

profile of v4, /device:TPU:20, one launch (start us, length us, event | category | flops | bytes accessed | tf_op | source)
XLA Modules:
  0.0 225.0 jit_solution(14703264385746569761)
XLA Ops:
  0.0 0.7 stack.9
  0.7 0.7 stack.10
  1.5 0.8 pad_maximum_fusion
  2.3 0.2 copy.18
  2.5 0.8 pad.8.wdt_ref
  3.3 0.0 copy-start.4
  3.3 0.0 copy-start.5
  3.3 0.0 copy-start.6
  3.3 0.0 copy-start.7
  3.3 135.1 %shard_map.118 = (bf16[528,1280]{1,0:T(8,128)(2,1)}, f32[528,128]{1,0:T(8,128)}, bf16[528,1280]{1,0:T(8,128)(2,1)}, s32[8,8,256]{2,1,0:T(8,128)}) custom-call(bf16[256,4096]{1,0:T(8,128)(2,1)} %tok_hbm.1, s32[1,256]{1,0:T(1,128)} %bitcast.12, s32[1,256]{1,0:T(1,128)} %bitcast.13, bf16[512,5120]{1,0:T(8,128)(2,1)} %w_hbm.2, bf16[2,512,128]{2,1,0:T(8,128)(2,1)} %pad.8.wdt_ref), custom_call_target="tpu_custom_call" | custom-call | tf_op jit(solution)/shard_map/pallas_call | solution.py:466
  138.4 0.0 copy-done.4
  138.4 0.0 copy-done.5
  138.5 0.0 copy-done.6
  138.5 0.0 copy-done.7
  138.5 0.0 copy-start
  138.5 1.3 copy-done
  139.8 0.0 copy-start.1
  139.8 1.3 copy-done.1
  141.1 0.0 copy-start.2
  141.1 1.0 copy-done.2
  142.1 0.0 copy-start.3
  142.1 0.8 copy-done.3
  142.9 37.8 %shard_map.119.normed_ref = bf16[512,1024]{1,0:T(8,128)(2,1)S(1)} custom-call(bf16[528,1280]{1,0:T(8,128)(2,1)S(1)} %copy-done, f32[528,128]{1,0:T(8,128)S(1)} %copy-done.2, bf16[528,1280]{1,0:T(8,128)(2,1)S(1)} %copy-done.1, s32[8,8,256]{2,1,0:T(8,128)S(1)} %copy-done.3, f32[4,2048]{1,0:T(4,128)S(1)} %copy-done.4, f32[4,2,512]{2,1,0:T(2,128)S(1)} %copy-done.5, ...), custom_call_target="tpu_custom_call" | custom-call | tf_op jit(solution)/shard_map/pallas_call | solution.py:832
  180.7 43.4 %shard_map.120 = bf16[64,4096]{1,0:T(8,128)(2,1)S(1)} custom-call(bf16[512,1024]{1,0:T(8,128)(2,1)S(1)} %shard_map.119.normed_ref, bf16[4096,2048]{1,0:T(8,128)(2,1)} %w_hbm.3), custom_call_target="tpu_custom_call" | custom-call | tf_op jit(solution)/shard_map/pallas_call | solution.py:612
  224.2 0.8 copy.22
  (2 shorter events, 0.0 us)
Async XLA Ops:
  3.3 135.2 %copy-start.4 = (f32[4,2048]{1,0:T(4,128)S(1)}, f32[4,2048]{1,0:T(4,128)}, u32[]{:S(2)}) copy-start(f32[4,2048]{1,0:T(4,128)} %tapx_ref.1) | copy-start | bytes 98308
  3.3 135.2 %copy-start.5 = (f32[4,2,512]{2,1,0:T(2,128)S(1)}, f32[4,2,512]{2,1,0:T(2,128)}, u32[]{:S(2)}) copy-start(f32[4,2,512]{2,1,0:T(2,128)} %tapbc_ref.1) | copy-start | bytes 49156
  3.3 135.2 %copy-start.6 = (f32[2048]{0:T(1024)S(1)}, f32[2048]{0:T(1024)}, u32[]{:S(2)}) copy-start(f32[2048]{0:T(1024)} %param.23) | copy-start | bytes 24580
  3.3 135.2 %copy-start.7 = (f32[32]{0:T(128)S(1)}, f32[32]{0:T(128)}, u32[]{:S(2)}) copy-start(f32[32]{0:T(128)} %skip_ref.1) | copy-start | bytes 388
  138.5 1.3 copy-start
  139.8 1.3 copy-start.1
  141.1 1.0 copy-start.2
  142.1 0.8 copy-start.3
